TPU v7x, 512 devices: a whole 4x4x16 slice. The times are simulated.
512 devices in a mesh: blk: 4 (over x_lo, core), grp: 128 (over x_hi, y, z).
Axes of the slice: x: 4 (x_hi: 2, x_lo: 2; x = x_hi * 2 + x_lo), y: 4, z: 16, core: 2. Of those that a mesh axis runs over, the one named last changes fastest.
Arguments:
- text: bfloat16 [512, 512], P(('blk', 'grp')), may hold values from -20 to 20
- keys: bfloat16 [512, 196, 512], P(('blk', 'grp')), may hold values from -400 to 400
- values: bfloat16 [512, 196, 512], P(('blk', 'grp')), may hold values from -5 to 5
- pair_image: int32 [512], replicated, may hold values from 0 to 511, each once
Outputs:
- caption_loss: float32 [512], P(('blk', 'grp'))
- grad_text: float32 [512, 512], P(('blk', 'grp'))
- grad_keys: float32 [512, 196, 512], P(('blk', 'grp'))
- grad_values: float32 [512, 196, 512], P(('blk', 'grp'))
All inputs are finite; a program needn't handle non-finite values.
Results may differ from a plain program's by a relative error of at most 0.008.
Values may be sent and summed in bfloat16 or wider, within the bound.
No kernel may reach another device: no remote copies, remote signals or barrier semaphores. Data moves between devices by JAX's collectives and lax.ppermute only.
A program may use at most 64 MiB of HBM per device.

v0:
```python
import jax
import jax.numpy as jnp
from jax import lax
from jax.sharding import Mesh
from jax.sharding import PartitionSpec as P

HEADS = 8
GRP = ("grp_0", "grp_1", "grp_2")
BLK_GRP = ("blk", "grp_0", "grp_1", "grp_2")


EPS = 1e-06
LOGIT_SCALE = 10.0
LOGIT_BIAS = -1.0


def joined_along(parts, dim):
    shape = list(parts.shape[1:])
    shape[dim] *= parts.shape[0]
    return jnp.moveaxis(parts, 0, dim).reshape(shape)


def stacked_from(shard, axes, turns):
    parts = shard[None]
    for k in turns:
        parts = lax.all_gather(parts, axes[k], axis=0, tiled=True)
    held = [lax.axis_size(axes[k]) for k in reversed(turns)]
    parts = parts.reshape(*held, *shard.shape)
    turned = sorted(range(len(turns)), key=lambda place: turns[len(turns) - 1 - place])
    return parts.transpose(*turned, *range(len(turns), parts.ndim)).reshape(-1, *shard.shape)


def gather_axes(shard, axes, turns, dim):
    return joined_along(stacked_from(shard, axes, turns), dim)


def passed_along(block, axis, distance):
    devices = range(lax.axis_size(axis))
    route = [((i - distance) % len(devices), i) for i in devices]
    return lax.ppermute(block, axis, route)


def cut_along(shard, dim, length):
    before, after = (shard.shape[:dim], shard.shape[dim + 1 :])
    return jnp.moveaxis(shard.reshape(*before, length, -1, *after), dim, 0)


def summed_on_arrival(shard, axis, dim):
    parts = cut_along(shard, dim, lax.axis_size(axis))
    arrived = lax.all_to_all(parts, axis, split_axis=0, concat_axis=0, tiled=True)
    return arrived.astype(jnp.float32).sum(axis=0)


def sum_by_axis(shard, axes, dim):
    far, near = axes
    own = summed_on_arrival(cut_along(shard, dim, lax.axis_size(far)), near, dim + 1)
    return jnp.sum(
        lax.all_to_all(own.astype(jnp.bfloat16), far, 0, 0, tiled=True).astype(jnp.float32), axis=0
    )


def image_terms(block_text, normed, tnorm, pairs, image_id, keys_one, values_one):
    count = block_text.shape[0]
    width = block_text.shape[1]
    depth = width // HEADS
    queries = block_text.reshape(count, HEADS, depth)
    patch_keys = keys_one.reshape(-1, HEADS, depth)
    patch_values = values_one.reshape(-1, HEADS, depth)
    scores = jnp.einsum(
        "chd,phd->chp", queries, patch_keys, preferred_element_type=jnp.float32
    ) * depth ** (-0.5)
    weights = jax.nn.softmax(scores, axis=-1)
    attn = weights.astype(jnp.bfloat16)
    pooled = jnp.einsum(
        "chp,phd->chd", attn, patch_values, preferred_element_type=jnp.float32
    ).reshape(count, width)
    pnorm = lax.rsqrt(jnp.mean(pooled * pooled, -1, keepdims=True) + EPS)
    unit = pooled * pnorm
    cosine = jnp.mean(unit * normed, -1)
    logit = LOGIT_SCALE * cosine + LOGIT_BIAS
    label = jnp.where(pairs == image_id, 1.0, -1.0).astype(jnp.float32)
    loss = jax.nn.softplus(-label * logit)
    slope = -label * jax.nn.sigmoid(-label * logit)
    dcos = LOGIT_SCALE / width * slope[:, None]
    dunit = dcos * normed
    dnormed = dcos * unit
    dpool = pnorm * (dunit - unit * jnp.mean(dunit * unit, -1, keepdims=True))
    dout = dpool.astype(jnp.bfloat16).reshape(count, HEADS, depth)
    dattn = jnp.einsum("chd,phd->chp", dout, patch_values, preferred_element_type=jnp.float32)
    grad_v = jnp.einsum("chp,chd->phd", attn, dout, preferred_element_type=jnp.float32).reshape(
        -1, width
    )
    dscore = (
        weights * (dattn - jnp.sum(weights * dattn, -1, keepdims=True)) * depth ** (-0.5)
    ).astype(jnp.bfloat16)
    grad_q = jnp.einsum(
        "chp,phd->chd", dscore, patch_keys, preferred_element_type=jnp.float32
    ).reshape(count, width)
    grad_k = jnp.einsum(
        "chp,chd->phd", dscore, queries, preferred_element_type=jnp.float32
    ).reshape(-1, width)
    grad_x = grad_q + tnorm * (dnormed - normed * jnp.mean(dnormed * normed, -1, keepdims=True))
    return (loss, grad_x, grad_k, grad_v)


def pair_block(block_text, pair_image, first_caption, keys, values, first_image):
    count = block_text.shape[0]
    width = block_text.shape[1]
    text_wide = block_text.astype(jnp.float32)
    tnorm = lax.rsqrt(jnp.mean(text_wide * text_wide, -1, keepdims=True) + EPS)
    normed = text_wide * tnorm
    pairs = lax.dynamic_slice_in_dim(pair_image, first_caption, count)
    image_ids = first_image + jnp.arange(keys.shape[0], dtype=jnp.int32)

    def one_image(carry, item):
        keys_one, values_one, image_id = item
        loss, grad_x, grad_k, grad_v = image_terms(
            block_text, normed, tnorm, pairs, image_id, keys_one, values_one
        )
        return ((carry[0] + loss, carry[1] + grad_x), (grad_k, grad_v))

    start = (jnp.zeros((count,), jnp.float32), jnp.zeros((count, width), jnp.float32))
    (loss_sum, grad_text), (grad_keys, grad_values) = lax.scan(
        one_image, start, (keys, values, image_ids)
    )
    return (loss_sum, grad_text, grad_keys, grad_values)


def local(text, keys, values, pair_image):
    per_device = keys.shape[0]
    groups = lax.axis_size("blk")
    members = lax.axis_size(GRP)
    group_index = lax.axis_index("blk")
    first_image = (group_index * members + lax.axis_index(GRP)) * per_device
    image_total = per_device * groups * members
    group_text = gather_axes(text, GRP, (0, 1, 2), 0)
    span = group_text.shape[0]
    carried = (jnp.zeros((span,), jnp.float32), jnp.zeros((span, text.shape[1]), jnp.float32))
    grad_keys = jnp.zeros(keys.shape, jnp.float32)
    grad_values = jnp.zeros(values.shape, jnp.float32)
    for turn in range(groups):
        source = (group_index - turn) % groups
        loss_part, grad_part, keys_part, values_part = pair_block(
            group_text, pair_image, source * span, keys, values, first_image
        )
        carried = (carried[0] + loss_part, carried[1] + grad_part)
        grad_keys = grad_keys + keys_part
        grad_values = grad_values + values_part
        if turn + 1 < groups:
            group_text = passed_along(group_text, "blk", 1)
        carried = (
            passed_along(carried[0].astype(jnp.bfloat16), "blk", 1).astype(jnp.float32),
            passed_along(carried[1].astype(jnp.bfloat16), "blk", 1).astype(jnp.float32),
        )
    loss_own, grad_own = (
        sum_by_axis(carried[0].astype(jnp.bfloat16), ("grp_0", ("grp_1", "grp_2")), 0),
        sum_by_axis(carried[1].astype(jnp.bfloat16), ("grp_0", ("grp_1", "grp_2")), 0),
    )
    return (loss_own / image_total, grad_own, grad_keys, grad_values)


def solution(mesh):
    torus = Mesh(
        mesh.devices.reshape(mesh.shape["blk"], 2, 4, 16), ("blk", "grp_0", "grp_1", "grp_2")
    )
    in_specs = (P(BLK_GRP, None), P(BLK_GRP, None, None), P(BLK_GRP, None, None), P())
    out_specs = (P(BLK_GRP), P(BLK_GRP, None), P(BLK_GRP, None, None), P(BLK_GRP, None, None))
    return jax.shard_map(local, mesh=torus, in_specs=in_specs, out_specs=out_specs, check_vma=False)
```

profile of v0, /device:TPU:32, one launch (start us, length us, event | category | flops | bytes accessed | tf_op | source)
XLA Modules:
  0.0 177.8 jit_solution(3987377504278109835)
XLA Ops:
  0.7 1.1 copy.150
  1.7 5.8 %all-gather.3 = bf16[2,1,512]{2,1,0:T(2,128)(2,1)S(1)} all-gather(bf16[1,1,512]{2,1,0:T(2,128)(2,1)S(1)} %bitcast.258), channel_id=2, replica_groups=mesh['blk'=4,'grp_0'=2,'grp_1'=4,'grp_2'=16] {'grp_0'}, dimensions={0}, use_global_device_ids=true | all-gather | bytes 3072 | tf_op jit(solution)/shard_map/all_gather | solution.py:26
  7.6 11.2 %all-gather.4 = bf16[4,2,512]{2,1,0:T(2,128)(2,1)S(1)} all-gather(bf16[1,2,512]{2,1,0:T(2,128)(2,1)S(1)} %bitcast.257), channel_id=3, replica_groups=mesh['blk'=4,'grp_0'=2,'grp_1'=4,'grp_2'=16] {'grp_1'}, dimensions={0}, use_global_device_ids=true | all-gather | bytes 10240 | tf_op jit(solution)/shard_map/all_gather | solution.py:26
  18.8 34.0 %all-gather.2 = bf16[128,512]{1,0:T(8,128)(2,1)S(1)} all-gather(bf16[8,512]{1,0:T(8,128)(2,1)S(1)} %reshape.481), channel_id=4, replica_groups=mesh['blk'=4,'grp_0'=2,'grp_1'=4,'grp_2'=16] {'grp_2'}, dimensions={0}, use_global_device_ids=true | all-gather | bytes 139264 | tf_op jit(solution)/shard_map/all_gather | solution.py:26
  52.9 0.2 fusion.92
  53.5 0.7 copy-done
  54.4 0.5 fusion.179
  54.9 0.7 multiply_reduce_fusion.6
  55.9 0.6 copy-done.4
  56.6 1.9 %collective-permute-start = (bf16[128]{0:T(256)(128)(2,1)S(1)}, bf16[128]{0:T(256)(128)(2,1)S(1)}, u32[]{:S(2)}, u32[]{:S(2)}) collective-permute-start(bf16[128]{0:T(256)(128)(2,1)S(1)} %fusion.148), channel_id=1, source_target_pairs={{384,0},{0,128},{128,256},{256,384},{385,1},{1,129},{129,257},{257... | collective-permute-start | bytes 776 | tf_op jit(solution)/shard_map/ppermute | solution.py:40
  58.6 3.5 %collective-permute-start.1 = (bf16[128,512]{1,0:T(8,128)(2,1)S(1)}, bf16[128,512]{1,0:T(8,128)(2,1)S(1)}, u32[]{:S(2)}, u32[]{:S(2)}) collective-permute-start(bf16[128,512]{1,0:T(8,128)(2,1)S(1)} %bitcast.211), channel_id=1, source_target_pairs={{384,0},{0,128},{128,256},{256,384},{385,1},{1,129},{129,257},{257... | collective-permute-start | bytes 393224 | tf_op jit(solution)/shard_map/ppermute | solution.py:40
  62.5 0.2 copy.167
  63.0 0.6 fusion.122
  63.9 0.4 convolution_bitcast_fusion.3
  64.4 0.4 fusion.52
  65.3 1.9 %collective-permute-start.7 = (bf16[128,512]{1,0:T(8,128)(2,1)S(1)}, bf16[128,512]{1,0:T(8,128)(2,1)S(1)}, u32[]{:S(2)}, u32[]{:S(2)}) collective-permute-start(bf16[128,512]{1,0:T(8,128)(2,1)S(1)} %add_convert_fusion), channel_id=1, source_target_pairs={{384,0},{0,128},{128,256},{256,384},{385,1},{1,129},{129,257},{257... | collective-permute-start | bytes 393224 | tf_op jit(solution)/shard_map/ppermute | solution.py:40
  67.2 0.7 fusion.132
  67.9 1.3 fusion.51
  69.3 1.4 fusion.178
  70.7 0.7 fusion.121
  72.0 0.2 fusion.96
  72.5 0.4 convolution_bitcast_fusion.2
  72.9 1.5 convolution_add_fusion.2
  74.4 2.5 %collective-permute-start.2 = (bf16[128]{0:T(256)(128)(2,1)S(1)}, bf16[128]{0:T(256)(128)(2,1)S(1)}, u32[]{:S(2)}, u32[]{:S(2)}) collective-permute-start(bf16[128]{0:T(256)(128)(2,1)S(1)} %get-tuple-element.171), channel_id=1, source_target_pairs={{384,0},{0,128},{128,256},{256,384},{385,1},{1,129},{129,257},{257... | collective-permute-start | bytes 776 | tf_op jit(solution)/shard_map/ppermute | solution.py:40
  77.0 1.8 %fusion.46 = f32[8,128,64]{1,2,0:T(8,128)S(1)} fusion(bf16[196,8,64]{0,2,1:T(8,128)(2,1)S(1)} %bitcast.227, f32[128,8,196]{0,2,1:T(8,128)S(1)} %convolution_bitcast_fusion.2, f32[128,8,196]{0,2,1:T(8,128)} %get-tuple-element.197, f32[128,8]{0,1:T(8,128)S(1)} %get-tuple-element.196), kind=kOutput, calls=%fused_computation.58 | convolution fusion | flops 27096260 | bytes 2072576 | tf_op jit(solution)/shard_map/while/body/eval_jaxpr/chp,phd->chd/dot_general | solution.py:96
  79.2 1.9 %collective-permute-start.8 = (bf16[128,512]{1,0:T(8,128)(2,1)S(1)}, bf16[128,512]{1,0:T(8,128)(2,1)S(1)}, u32[]{:S(2)}, u32[]{:S(2)}) collective-permute-start(bf16[128,512]{1,0:T(8,128)(2,1)S(1)} %fusion.101), channel_id=1, source_target_pairs={{384,0},{0,128},{128,256},{256,384},{385,1},{1,129},{129,257},{257... | collective-permute-start | bytes 393224 | tf_op jit(solution)/shard_map/ppermute | solution.py:40
  81.1 3.5 %collective-permute-start.3 = (bf16[128,512]{1,0:T(8,128)(2,1)S(1)}, bf16[128,512]{1,0:T(8,128)(2,1)S(1)}, u32[]{:S(2)}, u32[]{:S(2)}) collective-permute-start(bf16[128,512]{1,0:T(8,128)(2,1)S(1)} %collective-permute-done.1), channel_id=1, source_target_pairs={{384,0},{0,128},{128,256},{256,384},{385,1},{1,129},{129,257},{257... | collective-permute-start | bytes 393224 | tf_op jit(solution)/shard_map/ppermute | solution.py:40
  84.6 2.7 %convolution_add_fusion.5 = f32[8,196,64]{1,2,0:T(8,128)} fusion(f32[8,196,64]{1,2,0:T(8,128)S(1)} %copy-done.5, bf16[128,8,64]{0,2,1:T(8,128)(2,1)S(1)} %bitcast.254, f32[128,8,196]{0,2,1:T(8,128)S(1)} %convolution_bitcast_fusion.2, f32[128,8,196]{0,2,1:T(8,128)} %get-tuple-element.197, f32[128,8]{0,1:T(8,128)S(1)} %get-tuple-element.196), kind=kOutput, calls=%fused_computation.49 | convolution fusion | flops 27196612 | bytes 2543616 | tf_op jit(solution)/shard_map/while/body/eval_jaxpr/chp,chd->phd/dot_general | solution.py:99
  87.5 1.4 fusion.177
  88.9 0.7 fusion.120
  90.7 1.9 %collective-permute-start.4 = (bf16[128]{0:T(256)(128)(2,1)S(1)}, bf16[128]{0:T(256)(128)(2,1)S(1)}, u32[]{:S(2)}, u32[]{:S(2)}) collective-permute-start(bf16[128]{0:T(256)(128)(2,1)S(1)} %get-tuple-element.173), channel_id=1, source_target_pairs={{384,0},{0,128},{128,256},{256,384},{385,1},{1,129},{129,257},{257... | collective-permute-start | bytes 776 | tf_op jit(solution)/shard_map/ppermute | solution.py:40
  92.6 0.4 convolution_bitcast_fusion.1
  93.0 1.8 %fusion.41 = f32[8,128,64]{1,2,0:T(8,128)S(1)} fusion(bf16[196,8,64]{0,2,1:T(8,128)(2,1)S(1)} %bitcast.230, f32[128,8,196]{0,2,1:T(8,128)S(1)} %convolution_bitcast_fusion.1, f32[128,8,196]{0,2,1:T(8,128)} %get-tuple-element.193, f32[128,8]{0,1:T(8,128)S(1)} %get-tuple-element.192), kind=kOutput, calls=%fused_computation.54 | convolution fusion | flops 27096260 | bytes 2072576 | tf_op jit(solution)/shard_map/while/body/eval_jaxpr/chp,phd->chd/dot_general | solution.py:96
  95.0 3.5 %collective-permute-start.5 = (bf16[128,512]{1,0:T(8,128)(2,1)S(1)}, bf16[128,512]{1,0:T(8,128)(2,1)S(1)}, u32[]{:S(2)}, u32[]{:S(2)}) collective-permute-start(bf16[128,512]{1,0:T(8,128)(2,1)S(1)} %collective-permute-done.3), channel_id=1, source_target_pairs={{384,0},{0,128},{128,256},{256,384},{385,1},{1,129},{129,257},{257... | collective-permute-start | bytes 393224 | tf_op jit(solution)/shard_map/ppermute | solution.py:40
  98.8 2.1 %collective-permute-start.9 = (bf16[128,512]{1,0:T(8,128)(2,1)S(1)}, bf16[128,512]{1,0:T(8,128)(2,1)S(1)}, u32[]{:S(2)}, u32[]{:S(2)}) collective-permute-start(bf16[128,512]{1,0:T(8,128)(2,1)S(1)} %fusion.109), channel_id=1, source_target_pairs={{384,0},{0,128},{128,256},{256,384},{385,1},{1,129},{129,257},{257... | collective-permute-start | bytes 393224 | tf_op jit(solution)/shard_map/ppermute | solution.py:40
  100.9 0.4 collective-permute-done.5
  101.5 1.4 fusion.176
  102.9 0.7 fusion.119
  104.6 0.4 convolution_bitcast_fusion
  105.1 1.8 %fusion.36 = f32[8,128,64]{1,2,0:T(8,128)S(1)} fusion(bf16[196,8,64]{0,2,1:T(8,128)(2,1)S(1)} %bitcast.233, f32[128,8,196]{0,2,1:T(8,128)S(1)} %convolution_bitcast_fusion, f32[128,8,196]{0,2,1:T(8,128)} %get-tuple-element.177, f32[128,8]{0,1:T(8,128)S(1)} %get-tuple-element.176), kind=kOutput, calls=%fused_computation.50 | convolution fusion | flops 27096260 | bytes 2072576 | tf_op jit(solution)/shard_map/while/body/eval_jaxpr/chp,phd->chd/dot_general | solution.py:96
  107.1 2.1 %collective-permute-start.6 = (bf16[128]{0:T(256)(128)(2,1)S(1)}, bf16[128]{0:T(256)(128)(2,1)S(1)}, u32[]{:S(2)}, u32[]{:S(2)}) collective-permute-start(bf16[128]{0:T(256)(128)(2,1)S(1)} %get-tuple-element.175), channel_id=1, source_target_pairs={{384,0},{0,128},{128,256},{256,384},{385,1},{1,129},{129,257},{257... | collective-permute-start | bytes 776 | tf_op jit(solution)/shard_map/ppermute | solution.py:40
  109.3 3.3 %collective-permute-start.10 = (bf16[128,512]{1,0:T(8,128)(2,1)S(1)}, bf16[128,512]{1,0:T(8,128)(2,1)S(1)}, u32[]{:S(2)}, u32[]{:S(2)}) collective-permute-start(bf16[128,512]{1,0:T(8,128)(2,1)S(1)} %fusion.117), channel_id=1, source_target_pairs={{384,0},{0,128},{128,256},{256,384},{385,1},{1,129},{129,257},{257... | collective-permute-start | bytes 393224 | tf_op jit(solution)/shard_map/ppermute | solution.py:40
  112.8 0.7 copy.163
  113.5 10.9 %all-to-all-start = ((bf16[64,2,1]{1,2,0:T(2,128)(2,1)}), bf16[64,2,1]{1,2,0:T(2,128)(2,1)S(1)}, u32[]{:S(2)}, u32[]{:S(2)}) async-start(bf16[64,2,1]{1,2,0:T(2,128)(2,1)} %copy.163), calls=%async_computation | async-start | bytes 65536 | tf_op jit(solution)/shard_map/all_to_all | solution.py:50
  124.5 1.7 convolution_add_fusion.1
  126.2 0.8 copy.179
  127.0 10.9 %all-to-all-done = bf16[64,2,1]{1,2,0:T(2,128)(2,1)S(1)} async-done(((bf16[64,2,1]{1,2,0:T(2,128)(2,1)}), bf16[64,2,1]{1,2,0:T(2,128)(2,1)S(1)}, u32[]{:S(2)}, u32[]{:S(2)}) %all-to-all-start) | async-done | bytes 288 | tf_op jit(solution)/shard_map/all_to_all | solution.py:50
  137.8 5.5 %all-to-all-start.2 = ((bf16[64,2,1,512]{3,1,2,0:T(2,128)(2,1)}), bf16[64,2,1,512]{3,1,2,0:T(2,128)(2,1)S(1)}, u32[]{:S(2)}, u32[]{:S(2)}) async-start(bf16[64,2,1,512]{3,1,2,0:T(2,128)(2,1)} %copy.179), calls=%async_computation.2 | async-start | bytes 262144 | tf_op jit(solution)/shard_map/all_to_all | solution.py:50
  143.3 2.8 %convolution_add_fusion.4 = f32[8,196,64]{1,2,0:T(8,128)} fusion(f32[8,196,64]{1,2,0:T(8,128)} %convolution_add_fusion.5, bf16[128,8,64]{0,2,1:T(8,128)(2,1)S(1)} %bitcast.246, f32[128,8,196]{0,2,1:T(8,128)S(1)} %convolution_bitcast_fusion.1, f32[128,8,196]{0,2,1:T(8,128)} %get-tuple-element.193, f32[128,8]{0,1:T(8,128)S(1)} %get-tuple-element.192), kind=kOutput, calls=%fused_computation.48 | convolution fusion | flops 27196612 | bytes 2543616 | tf_op jit(solution)/shard_map/while/body/eval_jaxpr/chp,chd->phd/dot_general | solution.py:99
  146.2 0.7 convolution_add_fusion
  146.8 1.0 copy.183
  147.9 1.9 %convolution_add_fusion.3 = f32[8,196,64]{1,2,0:T(8,128)S(1)} fusion(f32[8,196,64]{1,2,0:T(8,128)S(1)} %copy-done.6, bf16[128,8,64]{0,2,1:T(8,128)(2,1)S(1)} %bitcast.250, f32[128,8,196]{0,2,1:T(8,128)S(1)} %convolution_bitcast_fusion, f32[128,8,196]{0,2,1:T(8,128)} %get-tuple-element.177, f32[128,8]{0,1:T(8,128)S(1)} %get-tuple-element.176), kind=kOutput, calls=%fused_computation.47 | convolution fusion | flops 27196612 | bytes 2543616 | tf_op jit(solution)/shard_map/while/body/eval_jaxpr/chp,chd->phd/dot_general | solution.py:99
  149.7 1.0 copy.182
  150.8 0.7 copy.164
  151.5 7.0 %all-to-all-done.2 = bf16[64,2,1,512]{3,1,2,0:T(2,128)(2,1)S(1)} async-done(((bf16[64,2,1,512]{3,1,2,0:T(2,128)(2,1)}), bf16[64,2,1,512]{3,1,2,0:T(2,128)(2,1)S(1)}, u32[]{:S(2)}, u32[]{:S(2)}) %all-to-all-start.2) | async-done | bytes 131104 | tf_op jit(solution)/shard_map/all_to_all | solution.py:50
  158.5 4.0 %all-to-all-start.1 = ((bf16[2,1,1]{2,1,0:T(2,128)(2,1)}), bf16[2,1,1]{2,1,0:T(2,128)(2,1)S(1)}, u32[]{:S(2)}, u32[]{:S(2)}) async-start(bf16[2,1,1]{2,1,0:T(2,128)(2,1)} %copy.164), calls=%async_computation.1 | async-start | bytes 2048 | tf_op jit(solution)/shard_map/all_to_all | solution.py:58
  162.7 0.5 broadcast.463
  163.2 0.7 reduce.15
  163.8 0.6 reshape.483
  164.4 3.2 %all-to-all-done.1 = bf16[2,1,1]{2,1,0:T(2,128)(2,1)S(1)} async-done(((bf16[2,1,1]{2,1,0:T(2,128)(2,1)}), bf16[2,1,1]{2,1,0:T(2,128)(2,1)S(1)}, u32[]{:S(2)}, u32[]{:S(2)}) %all-to-all-start.1) | async-done | bytes 36 | tf_op jit(solution)/shard_map/all_to_all | solution.py:58
  167.6 3.2 %all-to-all-start.3 = ((bf16[2,2,256]{2,1,0:T(2,128)(2,1)}), bf16[2,2,256]{2,1,0:T(2,128)(2,1)S(1)}, u32[]{:S(2)}, u32[]{:S(2)}) async-start(bf16[2,2,256]{2,1,0:T(2,128)(2,1)} %reshape.483), calls=%async_computation.3 | async-start | bytes 4096 | tf_op jit(solution)/shard_map/all_to_all | solution.py:58
  170.8 0.6 convert_reduce_fusion.1
  172.1 4.0 %all-to-all-done.3 = bf16[2,2,256]{2,1,0:T(2,128)(2,1)S(1)} async-done(((bf16[2,2,256]{2,1,0:T(2,128)(2,1)}), bf16[2,2,256]{2,1,0:T(2,128)(2,1)S(1)}, u32[]{:S(2)}, u32[]{:S(2)}) %all-to-all-start.3) | async-done | bytes 2080 | tf_op jit(solution)/shard_map/all_to_all | solution.py:58
  176.1 0.6 convert_reduce_fusion
  (94 shorter events, 7.1 us)
Async XLA Ops:
  0.6 1.1 copy-start.3
  53.3 0.9 copy-start
  55.8 0.7 copy-start.4
  56.6 15.3 %collective-permute-start = (bf16[128]{0:T(256)(128)(2,1)S(1)}, bf16[128]{0:T(256)(128)(2,1)S(1)}, u32[]{:S(2)}, u32[]{:S(2)}) collective-permute-start(bf16[128]{0:T(256)(128)(2,1)S(1)} %fusion.148), channel_id=1, source_target_pairs={{384,0},{0,128},{128,256},{256,384},{385,1},{1,129},{129,257},{257... | collective-permute-start | bytes 776 | tf_op jit(solution)/shard_map/ppermute | solution.py:40
  58.6 10.6 %collective-permute-start.1 = (bf16[128,512]{1,0:T(8,128)(2,1)S(1)}, bf16[128,512]{1,0:T(8,128)(2,1)S(1)}, u32[]{:S(2)}, u32[]{:S(2)}) collective-permute-start(bf16[128,512]{1,0:T(8,128)(2,1)S(1)} %bitcast.211), channel_id=1, source_target_pairs={{384,0},{0,128},{128,256},{256,384},{385,1},{1,129},{129,257},{257... | collective-permute-start | bytes 393224 | tf_op jit(solution)/shard_map/ppermute | solution.py:40
  65.3 13.7 %collective-permute-start.7 = (bf16[128,512]{1,0:T(8,128)(2,1)S(1)}, bf16[128,512]{1,0:T(8,128)(2,1)S(1)}, u32[]{:S(2)}, u32[]{:S(2)}) collective-permute-start(bf16[128,512]{1,0:T(8,128)(2,1)S(1)} %add_convert_fusion), channel_id=1, source_target_pairs={{384,0},{0,128},{128,256},{256,384},{385,1},{1,129},{129,257},{257... | collective-permute-start | bytes 393224 | tf_op jit(solution)/shard_map/ppermute | solution.py:40
  74.4 15.6 %collective-permute-start.2 = (bf16[128]{0:T(256)(128)(2,1)S(1)}, bf16[128]{0:T(256)(128)(2,1)S(1)}, u32[]{:S(2)}, u32[]{:S(2)}) collective-permute-start(bf16[128]{0:T(256)(128)(2,1)S(1)} %get-tuple-element.171), channel_id=1, source_target_pairs={{384,0},{0,128},{128,256},{256,384},{385,1},{1,129},{129,257},{257... | collective-permute-start | bytes 776 | tf_op jit(solution)/shard_map/ppermute | solution.py:40
  79.0 5.7 %copy-start.5 = (f32[8,196,64]{1,2,0:T(8,128)S(1)}, f32[8,196,64]{1,2,0:T(8,128)}, u32[]{:S(2)}) copy-start(f32[8,196,64]{1,2,0:T(8,128)} %fusion.51) | copy-start | bytes 1204228
  79.2 19.4 %collective-permute-start.8 = (bf16[128,512]{1,0:T(8,128)(2,1)S(1)}, bf16[128,512]{1,0:T(8,128)(2,1)S(1)}, u32[]{:S(2)}, u32[]{:S(2)}) collective-permute-start(bf16[128,512]{1,0:T(8,128)(2,1)S(1)} %fusion.101), channel_id=1, source_target_pairs={{384,0},{0,128},{128,256},{256,384},{385,1},{1,129},{129,257},{257... | collective-permute-start | bytes 393224 | tf_op jit(solution)/shard_map/ppermute | solution.py:40
  81.1 6.3 %collective-permute-start.3 = (bf16[128,512]{1,0:T(8,128)(2,1)S(1)}, bf16[128,512]{1,0:T(8,128)(2,1)S(1)}, u32[]{:S(2)}, u32[]{:S(2)}) collective-permute-start(bf16[128,512]{1,0:T(8,128)(2,1)S(1)} %collective-permute-done.1), channel_id=1, source_target_pairs={{384,0},{0,128},{128,256},{256,384},{385,1},{1,129},{129,257},{257... | collective-permute-start | bytes 393224 | tf_op jit(solution)/shard_map/ppermute | solution.py:40
  90.7 13.3 %collective-permute-start.4 = (bf16[128]{0:T(256)(128)(2,1)S(1)}, bf16[128]{0:T(256)(128)(2,1)S(1)}, u32[]{:S(2)}, u32[]{:S(2)}) collective-permute-start(bf16[128]{0:T(256)(128)(2,1)S(1)} %get-tuple-element.173), channel_id=1, source_target_pairs={{384,0},{0,128},{128,256},{256,384},{385,1},{1,129},{129,257},{257... | collective-permute-start | bytes 776 | tf_op jit(solution)/shard_map/ppermute | solution.py:40
  95.0 6.3 %collective-permute-start.5 = (bf16[128,512]{1,0:T(8,128)(2,1)S(1)}, bf16[128,512]{1,0:T(8,128)(2,1)S(1)}, u32[]{:S(2)}, u32[]{:S(2)}) collective-permute-start(bf16[128,512]{1,0:T(8,128)(2,1)S(1)} %collective-permute-done.3), channel_id=1, source_target_pairs={{384,0},{0,128},{128,256},{256,384},{385,1},{1,129},{129,257},{257... | collective-permute-start | bytes 393224 | tf_op jit(solution)/shard_map/ppermute | solution.py:40
  98.8 10.4 %collective-permute-start.9 = (bf16[128,512]{1,0:T(8,128)(2,1)S(1)}, bf16[128,512]{1,0:T(8,128)(2,1)S(1)}, u32[]{:S(2)}, u32[]{:S(2)}) collective-permute-start(bf16[128,512]{1,0:T(8,128)(2,1)S(1)} %fusion.109), channel_id=1, source_target_pairs={{384,0},{0,128},{128,256},{256,384},{385,1},{1,129},{129,257},{257... | collective-permute-start | bytes 393224 | tf_op jit(solution)/shard_map/ppermute | solution.py:40
  101.5 1.4 copy-start.1
  107.1 5.6 %collective-permute-start.6 = (bf16[128]{0:T(256)(128)(2,1)S(1)}, bf16[128]{0:T(256)(128)(2,1)S(1)}, u32[]{:S(2)}, u32[]{:S(2)}) collective-permute-start(bf16[128]{0:T(256)(128)(2,1)S(1)} %get-tuple-element.175), channel_id=1, source_target_pairs={{384,0},{0,128},{128,256},{256,384},{385,1},{1,129},{129,257},{257... | collective-permute-start | bytes 776 | tf_op jit(solution)/shard_map/ppermute | solution.py:40
  109.3 16.9 %collective-permute-start.10 = (bf16[128,512]{1,0:T(8,128)(2,1)S(1)}, bf16[128,512]{1,0:T(8,128)(2,1)S(1)}, u32[]{:S(2)}, u32[]{:S(2)}) collective-permute-start(bf16[128,512]{1,0:T(8,128)(2,1)S(1)} %fusion.117), channel_id=1, source_target_pairs={{384,0},{0,128},{128,256},{256,384},{385,1},{1,129},{129,257},{257... | collective-permute-start | bytes 393224 | tf_op jit(solution)/shard_map/ppermute | solution.py:40
  113.5 24.3 %all-to-all-start = ((bf16[64,2,1]{1,2,0:T(2,128)(2,1)}), bf16[64,2,1]{1,2,0:T(2,128)(2,1)S(1)}, u32[]{:S(2)}, u32[]{:S(2)}) async-start(bf16[64,2,1]{1,2,0:T(2,128)(2,1)} %copy.163), calls=%async_computation | async-start | bytes 65536 | tf_op jit(solution)/shard_map/all_to_all | solution.py:50
  137.8 20.7 %all-to-all-start.2 = ((bf16[64,2,1,512]{3,1,2,0:T(2,128)(2,1)}), bf16[64,2,1,512]{3,1,2,0:T(2,128)(2,1)S(1)}, u32[]{:S(2)}, u32[]{:S(2)}) async-start(bf16[64,2,1,512]{3,1,2,0:T(2,128)(2,1)} %copy.179), calls=%async_computation.2 | async-start | bytes 262144 | tf_op jit(solution)/shard_map/all_to_all | solution.py:50
  143.3 2.8 %copy-start.2 = (bf16[128,512]{0,1:T(8,128)(2,1)S(1)}, bf16[128,512]{0,1:T(8,128)(2,1)}, u32[]{:S(2)}) copy-start(bf16[128,512]{0,1:T(8,128)(2,1)} %copy-done.1) | copy-start | bytes 393220
  146.8 1.0 copy-start.6
  158.5 9.1 %all-to-all-start.1 = ((bf16[2,1,1]{2,1,0:T(2,128)(2,1)}), bf16[2,1,1]{2,1,0:T(2,128)(2,1)S(1)}, u32[]{:S(2)}, u32[]{:S(2)}) async-start(bf16[2,1,1]{2,1,0:T(2,128)(2,1)} %copy.164), calls=%async_computation.1 | async-start | bytes 2048 | tf_op jit(solution)/shard_map/all_to_all | solution.py:58
  167.6 8.5 %all-to-all-start.3 = ((bf16[2,2,256]{2,1,0:T(2,128)(2,1)}), bf16[2,2,256]{2,1,0:T(2,128)(2,1)S(1)}, u32[]{:S(2)}, u32[]{:S(2)}) async-start(bf16[2,2,256]{2,1,0:T(2,128)(2,1)} %reshape.483), calls=%async_computation.3 | async-start | bytes 4096 | tf_op jit(solution)/shard_map/all_to_all | solution.py:58
where the time goes:
time: 179 us; the launch traced here: 178 us
  starting transfers between devices  51.9 us (29%)
  blocking collectives  51 us (28%)
  matrix products  28.3 us (16%)
  waiting for transfers between devices  25.6 us (14%)
  local copies, waits for them, and re-layouts  11.5 us (6%)
  other arithmetic  6.4 us (4%)
  between operations  3.09 us (2%)
    all_gather x3, blocking collectives, stacked_from(): parts = lax.all_gather(parts, axes[k], axis=0, tiled=True)  51 us
    ppermute x11, starting transfers between devices, passed_along(): return lax.ppermute(block, axis, route)  28.3 us
    all_to_all x2, waiting for transfers between devices, summed_on_arrival(): lax.all_to_all(parts, axis, split_axis=0, concat_axis=0, tiled=True)  17.8 us
    all_to_all x2, starting transfers between devices, summed_on_arrival(): lax.all_to_all(parts, axis, split_axis=0, concat_axis=0, tiled=True)  16.4 us
    dot_general x4, matrix products, image_terms(): jnp.einsum('chp,chd->phd', dscore, queries, preferred_element_type=jnp.fl...  8.6 us
    all_to_all x2, starting transfers between devices, sum_by_axis(): lax.all_to_all(own.astype(jnp.bfloat16), far, 0, 0, tiled=True)  7.24 us
    all_to_all x2, waiting for transfers between devices, sum_by_axis(): lax.all_to_all(own.astype(jnp.bfloat16), far, 0, 0, tiled=True)  7.2 us
    dot_general x4, matrix products, image_terms(): jnp.einsum('chp,phd->chd', dscore, patch_keys, preferred_element_type=jnp...  5.94 us
  transfers between devices with their start and end apart: 15, of which 6 were waited for; matrix products, arithmetic and copies ran while one was open for 23% of the time, Pallas kernels for 0%

commit v1 on v0

v1 whole, which is shorter than its diff:
```python
import jax
import jax.numpy as jnp
from jax import lax
from jax.sharding import Mesh
from jax.sharding import PartitionSpec as P

HEADS = 8
PLANE = ("blk", "row")
LINE = ("line",)


EPS = 1e-06
LOGIT_SCALE = 10.0
LOGIT_BIAS = -1.0


def gathered(shard, axes):
    held = lax.axis_size(axes)
    spread = jnp.broadcast_to(shard[None], (held, *shard.shape))
    return lax.all_to_all(spread, axes, 0, 0, tiled=True).reshape(-1, *shard.shape[1:])


def scattered_sum(rows, axes):
    held = lax.axis_size(axes)
    parts = rows.reshape(held, -1, rows.shape[1])
    arrived = lax.all_to_all(parts, axes, 0, 0, tiled=True)
    return jnp.sum(arrived.astype(jnp.float32), axis=0)


def image_terms(block_text, normed, tnorm, pairs, image_id, keys_one, values_one):
    count = block_text.shape[0]
    width = block_text.shape[1]
    depth = width // HEADS
    queries = block_text.reshape(count, HEADS, depth)
    patch_keys = keys_one.reshape(-1, HEADS, depth)
    patch_values = values_one.reshape(-1, HEADS, depth)
    scores = jnp.einsum(
        "chd,phd->chp", queries, patch_keys, preferred_element_type=jnp.float32
    ) * depth ** (-0.5)
    weights = jax.nn.softmax(scores, axis=-1)
    attn = weights.astype(jnp.bfloat16)
    pooled = jnp.einsum(
        "chp,phd->chd", attn, patch_values, preferred_element_type=jnp.float32
    ).reshape(count, width)
    pnorm = lax.rsqrt(jnp.mean(pooled * pooled, -1, keepdims=True) + EPS)
    unit = pooled * pnorm
    cosine = jnp.mean(unit * normed, -1)
    logit = LOGIT_SCALE * cosine + LOGIT_BIAS
    label = jnp.where(pairs == image_id, 1.0, -1.0).astype(jnp.float32)
    loss = jax.nn.softplus(-label * logit)
    slope = -label * jax.nn.sigmoid(-label * logit)
    dcos = LOGIT_SCALE / width * slope[:, None]
    dunit = dcos * normed
    dnormed = dcos * unit
    dpool = pnorm * (dunit - unit * jnp.mean(dunit * unit, -1, keepdims=True))
    dout = dpool.astype(jnp.bfloat16).reshape(count, HEADS, depth)
    dattn = jnp.einsum("chd,phd->chp", dout, patch_values, preferred_element_type=jnp.float32)
    grad_v = jnp.einsum("chp,chd->phd", attn, dout, preferred_element_type=jnp.float32).reshape(
        -1, width
    )
    dscore = (
        weights * (dattn - jnp.sum(weights * dattn, -1, keepdims=True)) * depth ** (-0.5)
    ).astype(jnp.bfloat16)
    grad_q = jnp.einsum(
        "chp,phd->chd", dscore, patch_keys, preferred_element_type=jnp.float32
    ).reshape(count, width)
    grad_k = jnp.einsum(
        "chp,chd->phd", dscore, queries, preferred_element_type=jnp.float32
    ).reshape(-1, width)
    grad_x = grad_q + tnorm * (dnormed - normed * jnp.mean(dnormed * normed, -1, keepdims=True))
    return (loss, grad_x, grad_k, grad_v)


def pair_block(block_text, pair_image, first_caption, keys, values, first_image):
    count = block_text.shape[0]
    width = block_text.shape[1]
    text_wide = block_text.astype(jnp.float32)
    tnorm = lax.rsqrt(jnp.mean(text_wide * text_wide, -1, keepdims=True) + EPS)
    normed = text_wide * tnorm
    pairs = lax.dynamic_slice_in_dim(pair_image, first_caption, count)
    image_ids = first_image + jnp.arange(keys.shape[0], dtype=jnp.int32)

    def one_image(carry, item):
        keys_one, values_one, image_id = item
        loss, grad_x, grad_k, grad_v = image_terms(
            block_text, normed, tnorm, pairs, image_id, keys_one, values_one
        )
        return ((carry[0] + loss, carry[1] + grad_x), (grad_k, grad_v))

    start = (jnp.zeros((count,), jnp.float32), jnp.zeros((count, width), jnp.float32))
    (loss_sum, grad_text), (grad_keys, grad_values) = lax.scan(
        one_image, start, (keys, values, image_ids)
    )
    return (loss_sum, grad_text, grad_keys, grad_values)


def local(text, keys, values, pair_image):
    image = lax.axis_index(PLANE + LINE)
    image_total = lax.axis_size(PLANE + LINE)
    all_text = gathered(gathered(text, LINE), PLANE)
    loss, grad, grad_keys, grad_values = pair_block(
        all_text, pair_image, 0, keys, values, image * keys.shape[0]
    )
    width = text.shape[1]
    sums = jnp.concatenate([grad, jnp.broadcast_to(loss[:, None], (loss.shape[0], 128))], axis=1)
    sums = scattered_sum(sums.astype(jnp.bfloat16), PLANE)
    sums = scattered_sum(sums, LINE)
    return (sums[:, width] / image_total, sums[:, :width], grad_keys, grad_values)


def solution(mesh):
    torus = Mesh(mesh.devices.reshape(4, 8, 16), ("blk", "row", "line"))
    over = PLANE + LINE
    in_specs = (P(over, None), P(over, None, None), P(over, None, None), P())
    out_specs = (P(over), P(over, None), P(over, None, None), P(over, None, None))
    return jax.shard_map(local, mesh=torus, in_specs=in_specs, out_specs=out_specs, check_vma=False)
```

time: 179 us -> 114 us (0.64)
  the two profiles are of different devices: /device:TPU:32 before, /device:TPU:1 now
where the time goes in v1:
time: 114 us; the launch traced here: 113 us
  blocking collectives  26.9 us (24%)
  matrix products  22.5 us (20%)
  waiting for transfers between devices  20.5 us (18%)
  starting transfers between devices  18.1 us (16%)
  local copies, waits for them, and re-layouts  17.9 us (16%)
  other arithmetic  4.03 us (4%)
  between operations  2.63 us (2%)
    all_to_all x1, blocking collectives, gathered(): lax.all_to_all(spread, axes, 0, 0, tiled=True).reshape(-1, *shard.shape[1:])  26.9 us
    all_to_all x2, waiting for transfers between devices, scattered_sum(): arrived = lax.all_to_all(parts, axes, 0, 0, tiled=True)  12.2 us
    all_to_all x1, starting transfers between devices, gathered(): lax.all_to_all(spread, axes, 0, 0, tiled=True).reshape(-1, *shard.shape[1:])  9.16 us
    all_to_all x2, starting transfers between devices, scattered_sum(): arrived = lax.all_to_all(parts, axes, 0, 0, tiled=True)  8.89 us
    all_to_all x1, waiting for transfers between devices, gathered(): lax.all_to_all(spread, axes, 0, 0, tiled=True).reshape(-1, *shard.shape[1:])  8.23 us
    dot_general x1, matrix products, image_terms(): jnp.einsum('chp,chd->phd', dscore, queries, preferred_element_type=jnp.fl...  6.15 us
    dot_general x1, matrix products, image_terms(): jnp.einsum('chp,phd->chd', dscore, patch_keys, preferred_element_type=jnp...  5.98 us
    unnamed x13, local copies, waits for them, and re-layouts  5.12 us
  transfers between devices with their start and end apart: 3, of which 3 were waited for; matrix products, arithmetic and copies ran while one was open for 12% of the time, Pallas kernels for 0%

profile of v1, /device:TPU:1, one launch (start us, length us, event | category | flops | bytes accessed | tf_op | source)
XLA Modules:
  0.0 112.6 jit_solution(16030268204567169331)
XLA Ops:
  0.6 0.7 reduce.6
  1.4 0.5 broadcast.183
  1.9 0.7 reduce.7
  2.6 26.9 %all_to_all.20 = bf16[16,2,256]{2,1,0:T(2,128)(2,1)S(1)} all-to-all(bf16[16,2,256]{2,1,0:T(2,128)(2,1)S(1)} %reshape.206), channel_id=1, replica_groups=mesh['blk'=4,'row'=8,'line'=16] {'line'}, dimensions={0} | all-to-all | bytes 32768 | tf_op jit(solution)/shard_map/all_to_all | solution.py:20
  29.6 0.8 broadcast_in_dim.64
  30.4 9.2 %all-to-all-start.1 = ((bf16[32,16,512]{2,1,0:T(8,128)(2,1)}), bf16[32,16,512]{2,1,0:T(8,128)(2,1)S(1)}, u32[]{:S(2)}, u32[]{:S(2)}) async-start(bf16[32,16,512]{2,1,0:T(8,128)(2,1)} %broadcast_in_dim.64), calls=%async_computation.1 | async-start | bytes 1048576 | tf_op jit(solution)/shard_map/all_to_all | solution.py:20
  39.6 1.1 copy.32
  40.7 0.0 copy-start.1
  40.7 1.2 %copy.34 = bf16[1,196,512]{1,2,0:T(8,128)(2,1)S(1)} copy(bf16[1,196,512]{2,1,0:T(8,128)(2,1)} %param.6) | data formatting | bytes 401408 | tf_op args[2]
  41.9 8.2 %all-to-all-done.1 = bf16[32,16,512]{2,1,0:T(8,128)(2,1)S(1)} async-done(((bf16[32,16,512]{2,1,0:T(8,128)(2,1)}), bf16[32,16,512]{2,1,0:T(8,128)(2,1)S(1)}, u32[]{:S(2)}, u32[]{:S(2)}) %all-to-all-start.1) | async-done | bytes 524320 | tf_op jit(solution)/shard_map/all_to_all | solution.py:20
  50.1 0.5 reshape_reshape.4
  50.6 0.7 copy.33
  51.4 2.9 %fusion.36 = (f32[512,8]{0,1:T(8,128)S(1)}, f32[512,8,196]{0,2,1:T(8,128)}) fusion(bf16[196,8,64]{0,2,1:T(8,128)(2,1)S(1)} %bitcast.65, bf16[512,8,64]{0,2,1:T(8,128)(2,1)S(1)} %copy.33), kind=kOutput, calls=%fused_computation.58 | convolution fusion | flops 105169088 | bytes 3952640 | tf_op jit(solution)/shard_map/while/body/eval_jaxpr/sub | solution.py:40
  54.3 0.0 copy-done.1
  54.3 2.4 %multiply_reduce_fusion.2 = (f32[512]{0:T(512)S(1)}, f32[512,8,64]{0,2,1:T(8,128)S(1)}) fusion(bf16[196,8,64]{0,2,1:T(8,128)(2,1)S(1)} %bitcast.61, f32[512,8,196]{0,2,1:T(8,128)} %get-tuple-element.61, f32[512,8]{0,1:T(8,128)S(1)} %get-tuple-element.60), kind=kOutput, calls=%fused_computation.35 | convolution fusion | flops 104889856 | bytes 4478976 | tf_op jit(solution)/shard_map/while/body/eval_jaxpr/chp,phd->chd/dot_general | solution.py:42
  56.7 0.0 copy-start.2
  56.7 0.2 fusion.23
  56.9 0.1 rsqrt.29
  57.0 2.0 %copy.36 = f32[512,8,64]{2,1,0:T(8,128)} copy(f32[512,8,64]{0,2,1:T(8,128)S(1)} %get-tuple-element.63) | data formatting | bytes 2097152 | tf_op jit(solution)/shard_map/while/body/eval_jaxpr/chp,phd->chd/transpose | solution.py:42
  59.0 0.1 rsqrt.30
  59.0 0.2 multiply_reduce_fusion.1
  59.3 0.0 copy-done.2
  59.3 0.1 mul.201
  59.4 1.9 %reshape.201 = f32[32,16,512]{2,1,0:T(8,128)S(1)} reshape(f32[512,8,64]{2,1,0:T(8,128)} %copy.36) | data formatting | bytes 2097152 | tf_op jit(solution)/shard_map/while/body/eval_jaxpr/reshape | solution.py:44
  61.3 0.4 fusion.18
  61.7 0.1 div.48
  61.8 0.4 multiply_reduce_fusion
  62.1 0.0 copy-start
  62.2 0.8 copy-done
  63.0 2.4 %fusion.37 = f32[8,512,196]{1,2,0:T(8,128)} fusion(bf16[512,8,64]{0,2,1:T(8,128)(2,1)S(1)} %get-tuple-element.59, bf16[196,8,64]{0,2,1:T(8,128)(2,1)S(1)} %bitcast.62), kind=kOutput, calls=%fused_computation.59 | convolution fusion | flops 102760448 | bytes 3936256 | tf_op jit(solution)/shard_map/while/body/eval_jaxpr/chd,phd->chp/dot_general | solution.py:57
  65.3 6.0 %fusion.14 = f32[512,8,64]{0,2,1:T(8,128)S(1)} fusion(bf16[196,8,64]{0,2,1:T(8,128)(2,1)} %bitcast.66, f32[8,512,196]{1,2,0:T(8,128)} %fusion.37, f32[512,8,196]{0,2,1:T(8,128)} %get-tuple-element.61, f32[512,8]{0,1:T(8,128)S(1)} %get-tuple-element.60), kind=kOutput, calls=%fused_computation.17 | convolution fusion | flops 108384448 | bytes 7688192 | tf_op jit(solution)/shard_map/while/body/eval_jaxpr/chp,phd->chd/dot_general | solution.py:64
  71.3 2.0 %copy.37 = f32[512,8,64]{2,1,0:T(8,128)} copy(f32[512,8,64]{0,2,1:T(8,128)S(1)} %fusion.14) | data formatting | bytes 2097152 | tf_op jit(solution)/shard_map/while/body/eval_jaxpr/chp,phd->chd/transpose | solution.py:64
  73.3 1.9 %reshape.202 = f32[32,16,512]{2,1,0:T(8,128)S(1)} reshape(f32[512,8,64]{2,1,0:T(8,128)} %copy.37) | data formatting | bytes 2097152 | tf_op jit(solution)/shard_map/while/body/eval_jaxpr/reshape | solution.py:66
  75.2 0.1 div.50
  75.3 0.1 reshape.204
  75.4 0.4 fusion.22
  75.8 0.1 broadcast_in_dim.69
  75.9 0.9 pad_maximum_fusion
  76.8 5.4 %all-to-all-start.2 = ((bf16[32,16,640]{2,1,0:T(8,128)(2,1)}), bf16[32,16,640]{2,1,0:T(8,128)(2,1)S(1)}, u32[]{:S(2)}, u32[]{:S(2)}) async-start(bf16[32,16,640]{2,1,0:T(8,128)(2,1)} %pad_maximum_fusion), calls=%async_computation.2 | async-start | bytes 1310720 | tf_op jit(solution)/shard_map/all_to_all | solution.py:26
  82.2 2.7 %fusion.24 = f32[8,64,196]{2,1,0:T(8,128)S(1)} fusion(bf16[512,8,64]{0,2,1:T(8,128)(2,1)} %copy-done, f32[512,8,196]{0,2,1:T(8,128)} %get-tuple-element.61, f32[512,8]{0,1:T(8,128)S(1)} %get-tuple-element.60), kind=kOutput, calls=%fused_computation.36 | convolution fusion | flops 104366080 | bytes 4153344 | tf_op jit(solution)/shard_map/while/body/eval_jaxpr/chp,chd->phd/dot_general | solution.py:58
  85.0 1.0 copy.40
  86.0 8.0 %all-to-all-done.2 = bf16[32,16,640]{2,1,0:T(8,128)(2,1)S(1)} async-done(((bf16[32,16,640]{2,1,0:T(8,128)(2,1)}), bf16[32,16,640]{2,1,0:T(8,128)(2,1)S(1)}, u32[]{:S(2)}, u32[]{:S(2)}) %all-to-all-start.2) | async-done | bytes 655392 | tf_op jit(solution)/shard_map/all_to_all | solution.py:26
  94.0 0.1 convert_reduce_fusion
  94.1 0.6 reshape.203
  94.7 3.5 %all-to-all-start.3 = ((f32[16,1,640]{2,1,0:T(1,128)}), f32[16,1,640]{2,1,0:T(1,128)S(1)}, u32[]{:S(2)}, u32[]{:S(2)}) async-start(f32[16,1,640]{2,1,0:T(1,128)} %reshape.203), calls=%async_computation.3 | async-start | bytes 81920 | tf_op jit(solution)/shard_map/all_to_all | solution.py:26
  98.2 6.2 %fusion.12 = f32[8,196,64]{1,2,0:T(8,128)S(1)} fusion(bf16[512,8,64]{0,2,1:T(8,128)(2,1)S(1)} %copy.33, f32[8,512,196]{1,2,0:T(8,128)} %fusion.37, f32[512,8,196]{0,2,1:T(8,128)} %get-tuple-element.61, f32[512,8]{0,1:T(8,128)S(1)} %get-tuple-element.60), kind=kOutput, calls=%fused_computation.15 | convolution fusion | flops 108384448 | bytes 7364608 | tf_op jit(solution)/shard_map/while/body/eval_jaxpr/chp,chd->phd/dot_general | solution.py:67
  104.4 1.0 copy.39
  105.4 4.3 %all-to-all-done.3 = f32[16,1,640]{2,1,0:T(1,128)S(1)} async-done(((f32[16,1,640]{2,1,0:T(1,128)}), f32[16,1,640]{2,1,0:T(1,128)S(1)}, u32[]{:S(2)}, u32[]{:S(2)}) %all-to-all-start.3) | async-done | bytes 40992 | tf_op jit(solution)/shard_map/all_to_all | solution.py:26
  109.7 0.6 slice.9
  110.3 0.5 slice.8
  (12 shorter events, 0.2 us)
Async XLA Ops:
  30.4 19.7 %all-to-all-start.1 = ((bf16[32,16,512]{2,1,0:T(8,128)(2,1)}), bf16[32,16,512]{2,1,0:T(8,128)(2,1)S(1)}, u32[]{:S(2)}, u32[]{:S(2)}) async-start(bf16[32,16,512]{2,1,0:T(8,128)(2,1)} %broadcast_in_dim.64), calls=%async_computation.1 | async-start | bytes 1048576 | tf_op jit(solution)/shard_map/all_to_all | solution.py:20
  40.7 13.6 %copy-start.1 = (bf16[1,196,512]{1,2,0:T(8,128)(2,1)}, bf16[1,196,512]{1,2,0:T(8,128)(2,1)S(1)}, u32[]{:S(2)}) copy-start(bf16[1,196,512]{1,2,0:T(8,128)(2,1)S(1)} %copy.32) | copy-start | bytes 602116
  56.7 2.6 %copy-start.2 = (s32[512]{0:T(512)S(1)}, s32[512]{0:T(512)}, u32[]{:S(2)}) copy-start(s32[512]{0:T(512)} %param.7) | copy-start | bytes 6148
  62.1 0.8 copy-start
  76.8 17.1 %all-to-all-start.2 = ((bf16[32,16,640]{2,1,0:T(8,128)(2,1)}), bf16[32,16,640]{2,1,0:T(8,128)(2,1)S(1)}, u32[]{:S(2)}, u32[]{:S(2)}) async-start(bf16[32,16,640]{2,1,0:T(8,128)(2,1)} %pad_maximum_fusion), calls=%async_computation.2 | async-start | bytes 1310720 | tf_op jit(solution)/shard_map/all_to_all | solution.py:26
  94.7 15.0 %all-to-all-start.3 = ((f32[16,1,640]{2,1,0:T(1,128)}), f32[16,1,640]{2,1,0:T(1,128)S(1)}, u32[]{:S(2)}, u32[]{:S(2)}) async-start(f32[16,1,640]{2,1,0:T(1,128)} %reshape.203), calls=%async_computation.3 | async-start | bytes 81920 | tf_op jit(solution)/shard_map/all_to_all | solution.py:26

commit v2 on v1

v2 whole, which is shorter than its diff:
```python
import functools

import jax
import jax.numpy as jnp
from jax import lax
from jax.experimental import pallas as pl
from jax.experimental.pallas import tpu as pltpu
from jax.sharding import Mesh
from jax.sharding import PartitionSpec as P

HEADS = 8
OVER = ("x_lo", "core", "x_hi", "y", "z")
PLANE = ("x_lo", "x_hi", "y")
LINE = ("core", "z")


EPS = 1e-06
LOGIT_SCALE = 10.0
LOGIT_BIAS = -1.0
LANES = 128
LOSS_LANES = 128
VMEM_BYTES = 24 << 20
SMALL_BYTES = 4 << 20


def exchanged(parts, axes):
    return lax.all_to_all(parts, axes, 0, 0, tiled=True)


def copies_kernel(row_ref, copies_ref):
    count, blocks, lanes = copies_ref.shape
    row = row_ref[...].astype(jnp.float32)
    cut = [row[:, lanes * block : lanes * (block + 1)] for block in range(blocks)]
    cut = jnp.concatenate(cut, axis=0).astype(jnp.bfloat16)
    copies_ref[...] = jnp.broadcast_to(cut[None], copies_ref.shape)


def rows_kernel(cut_ref, copies_ref):
    cut = cut_ref[...].astype(jnp.float32)
    rows = [cut[:, block] for block in range(cut.shape[1])]
    rows = jnp.concatenate(rows, axis=1).astype(jnp.bfloat16)
    copies_ref[...] = jnp.broadcast_to(rows[None], copies_ref.shape)


def total_kernel(image_total, parts_ref, loss_ref, grad_ref):
    width = grad_ref.shape[1]
    total = jnp.sum(parts_ref[...], axis=0)
    grad_ref[...] = total[:, :width]
    loss_ref[...] = total[:, width : width + 1] * (1.0 / image_total)


def gathered(row):
    width = row.shape[1]
    line, plane = lax.axis_size(LINE), lax.axis_size(PLANE)
    inside = pl.BlockSpec(memory_space=pltpu.VMEM)
    copies = pl.pallas_call(
        copies_kernel,
        out_shape=jax.ShapeDtypeStruct((line, width // LANES, LANES), row.dtype),
        in_specs=[inside],
        out_specs=inside,
        compiler_params=pltpu.CompilerParams(vmem_limit_bytes=SMALL_BYTES),
        name="copies",
    )(row)
    rows = pl.pallas_call(
        rows_kernel,
        out_shape=jax.ShapeDtypeStruct((plane, line, width), row.dtype),
        in_specs=[inside],
        out_specs=inside,
        compiler_params=pltpu.CompilerParams(vmem_limit_bytes=SMALL_BYTES),
        name="rows",
    )(exchanged(copies, LINE))
    return exchanged(rows, PLANE).reshape(-1, width)


def summed(rows, image_total, width):
    plane = PLANE + LINE[:1]
    parts = rows.reshape(lax.axis_size(plane), -1, rows.shape[1])
    parts = jnp.sum(exchanged(parts, plane).astype(jnp.float32), axis=0)
    parts = exchanged(parts[:, None], LINE[1:])
    inside = pl.BlockSpec(memory_space=pltpu.VMEM)
    return pl.pallas_call(
        functools.partial(total_kernel, image_total),
        out_shape=(
            jax.ShapeDtypeStruct((1, 1), jnp.float32),
            jax.ShapeDtypeStruct((1, width), jnp.float32),
        ),
        in_specs=[inside],
        out_specs=(inside, inside),
        compiler_params=pltpu.CompilerParams(vmem_limit_bytes=SMALL_BYTES),
        name="total",
    )(parts)


def gathered_place(caption, sizes):
    index = {}
    for axis, size in reversed(tuple(zip(OVER, sizes))):
        index[axis] = lax.rem(caption, size)
        caption = lax.div(caption, size)
    place = jnp.zeros_like(caption)
    for axis in PLANE + LINE:
        place = place * sizes[OVER.index(axis)] + index[axis]
    return place


def padded_head(rows, head):
    zeros = jnp.zeros_like(rows)
    return jnp.concatenate([rows, zeros] if head % 2 == 0 else [zeros, rows], axis=0)


def pair_of(head, depth):
    first = head // 2 * 2 * depth
    return slice(first, first + 2 * depth)


def pair_kernel(
    sizes, image_ref, pairs_ref, text_ref, keys_ref, values_ref,
    sums_ref, keys_out, values_out,
    keys_t_in, values_t_in,
    text_t, dout_t, attn, dscore, weights, pooled, grad_keys, grad_values, left,
):
    count, width = text_ref.shape
    patches = keys_ref.shape[0]
    depth = width // HEADS
    scale = depth ** (-0.5)
    text_t[...] = text_ref[...].T
    wide = text_t[...].astype(jnp.float32)
    tnorm = lax.rsqrt(jnp.mean(wide * wide, 0, keepdims=True) + EPS)
    values_t_in[...] = values_ref[...].T
    for head in range(HEADS):
        rows = slice(head * depth, (head + 1) * depth)
        query = text_t[rows, :] * jnp.asarray(scale, jnp.bfloat16)
        scores = jnp.dot(
            keys_ref[:, pair_of(head, depth)],
            padded_head(query, head),
            preferred_element_type=jnp.float32,
        )
        grown = jnp.exp(scores - jnp.max(scores, 0, keepdims=True))
        weight = grown * (1.0 / jnp.sum(grown, 0, keepdims=True))
        weights[head] = weight
        attn[head] = weight.astype(jnp.bfloat16)
        pooled[rows, :] = jnp.dot(
            values_t_in[rows, :], attn[head], preferred_element_type=jnp.float32
        )
    keys_t_in[...] = keys_ref[...].T
    pool = pooled[...]
    pnorm = lax.rsqrt(jnp.mean(pool * pool, 0, keepdims=True) + EPS)
    cosine = jnp.mean(pool * wide, 0, keepdims=True) * pnorm * tnorm
    logit = LOGIT_SCALE * cosine + LOGIT_BIAS
    captions = lax.broadcasted_iota(jnp.int32, (1, count), 1)
    described = jnp.where(pairs_ref[...] == image_ref[0], captions, 0)
    matching = gathered_place(jnp.sum(described, 1, keepdims=True), sizes)
    label = jnp.where(captions == matching, 1.0, -1.0).astype(jnp.float32)
    margin = -label * logit
    loss = jnp.maximum(margin, 0.0) + jnp.log1p(jnp.exp(-jnp.abs(margin)))
    slope = -label / (1.0 + jnp.exp(-margin))
    dcos = LOGIT_SCALE / width * slope
    dout_t[...] = (
        (pnorm * dcos * tnorm) * wide - (pnorm * dcos * cosine * pnorm) * pool
    ).astype(jnp.bfloat16)
    pooled[...] = (tnorm * dcos * pnorm) * pool - (tnorm * dcos * cosine * tnorm) * wide

    def over_captions(parts, rows_t, head):
        return lax.dot_general(
            parts[head],
            padded_head(rows_t[head * depth : (head + 1) * depth, :], head),
            (((1,), (1,)), ((), ())),
            preferred_element_type=jnp.float32,
        )

    blocks = HEADS // 2
    for block in range(blocks):
        lines = pl.ds(block, patches, stride=blocks)
        for head in (2 * block, 2 * block + 1):
            rows = slice(head * depth, (head + 1) * depth)
            dattn = jnp.dot(
                values_ref[:, pair_of(head, depth)],
                padded_head(dout_t[rows, :], head),
                preferred_element_type=jnp.float32,
            )
            weight = weights[head]
            carried = jnp.sum(weight * dattn, 0, keepdims=True)
            dscore[head] = (weight * scale * (dattn - carried)).astype(jnp.bfloat16)
            pooled[rows, :] += jnp.dot(
                keys_t_in[rows, :], dscore[head], preferred_element_type=jnp.float32
            )
        grad_values[lines, :] = over_captions(attn, dout_t, 2 * block) + over_captions(
            attn, dout_t, 2 * block + 1
        )
        grad_keys[lines, :] = over_captions(dscore, text_t, 2 * block) + over_captions(
            dscore, text_t, 2 * block + 1
        )
    values_copy = pltpu.make_async_copy(grad_values, values_out, left.at[0])
    keys_copy = pltpu.make_async_copy(grad_keys, keys_out, left.at[1])
    values_copy.start()
    keys_copy.start()
    sums_ref[:, :width] = pooled[...].T.astype(jnp.bfloat16)
    sums_ref[:, width:] = jnp.broadcast_to(loss, (LOSS_LANES, count)).T.astype(jnp.bfloat16)
    values_copy.wait()
    keys_copy.wait()


def one_image(sizes, image, pairs, all_text, keys, values):
    patches, width = keys.shape[1:]
    count = all_text.shape[0]
    flops = 2 * count * patches * width
    lines = (patches * HEADS // 2, 2 * width // HEADS)
    inside = pl.BlockSpec(memory_space=pltpu.VMEM)
    anywhere = pl.BlockSpec(memory_space=pl.ANY)
    tall_text = pltpu.VMEM((width, count), jnp.bfloat16)
    tall_image = pltpu.VMEM((width, patches), jnp.bfloat16)
    per_head = pltpu.VMEM((HEADS, patches, count), jnp.bfloat16)
    sums, grad_keys, grad_values = pl.pallas_call(
        functools.partial(pair_kernel, sizes),
        out_shape=(
            jax.ShapeDtypeStruct((count, width + LOSS_LANES), jnp.bfloat16),
            jax.ShapeDtypeStruct(lines, jnp.float32),
            jax.ShapeDtypeStruct(lines, jnp.float32),
        ),
        in_specs=[
            pl.BlockSpec(memory_space=pltpu.SMEM),
            *[inside] * 4,
        ],
        out_specs=(inside, anywhere, anywhere),
        scratch_shapes=[
            tall_image,
            tall_image,
            tall_text,
            tall_text,
            per_head,
            per_head,
            pltpu.VMEM((HEADS, patches, count), jnp.float32),
            pltpu.VMEM((width, count), jnp.float32),
            pltpu.VMEM(lines, jnp.float32),
            pltpu.VMEM(lines, jnp.float32),
            pltpu.SemaphoreType.DMA((2,)),
        ],
        compiler_params=pltpu.CompilerParams(vmem_limit_bytes=VMEM_BYTES),
        cost_estimate=pl.CostEstimate(
            flops=6 * flops, bytes_accessed=3 << 20, transcendentals=HEADS * patches * count
        ),
        name="pairs",
    )(image, pairs, all_text, keys[0], values[0])
    return sums, grad_keys.reshape(keys.shape), grad_values.reshape(values.shape)


def local(text, keys, values, pair_image):
    width = text.shape[1]
    image = lax.axis_index(OVER)
    image_total = lax.axis_size(OVER)
    all_text = gathered(text)
    sums, grad_keys, grad_values = one_image(
        tuple(lax.axis_size(axis) for axis in OVER),
        image.astype(jnp.int32).reshape(1),
        pair_image.reshape(1, -1),
        all_text,
        keys,
        values,
    )
    loss, grad_text = summed(sums, image_total, width)
    return (loss.reshape(1), grad_text, grad_keys, grad_values)


def solution(mesh):
    torus = Mesh(mesh.devices.reshape(2, 2, 2, 4, 16), OVER)
    in_specs = (P(OVER, None), P(OVER, None, None), P(OVER, None, None), P())
    out_specs = (P(OVER), P(OVER, None), P(OVER, None, None), P(OVER, None, None))
    return jax.shard_map(local, mesh=torus, in_specs=in_specs, out_specs=out_specs, check_vma=False)
```

time: 114 us -> 88.5 us (0.78)
  blocking collectives: 26.9 us -> 60.9 us
  matrix products: 22.5 us -> 0 us
  local copies, waits for them, and re-layouts: 17.9 us -> 0.71 us
  starting transfers between devices: 18.1 us -> 6.89 us
  waiting for transfers between devices: 20.5 us -> 10.7 us
  Pallas kernels: 0 us -> 8.15 us
  other arithmetic: 4.03 us -> 0.1 us
  between operations: 2.63 us -> 0.68 us
    all_to_all x1 -> x3, blocking collectives: 26.9 us -> 60.9 us  [exchanged(): return lax.all_to_all(parts, axes, 0, 0, tiled=True)]
    dot_general x5 -> x0, matrix products: 19.6 us -> none  [the longest x1 6.15 us: image_terms(): jnp.einsum('chp,chd->phd', dscore, queries, preferred_element_type=jnp.fl...]
    all_to_all x3 -> x1, starting transfers between devices: 18.1 us -> 6.89 us  [exchanged(): return lax.all_to_all(parts, axes, 0, 0, tiled=True)]
    all_to_all x3 -> x1, waiting for transfers between devices: 20.5 us -> 10.7 us  [exchanged(): return lax.all_to_all(parts, axes, 0, 0, tiled=True)]
    pallas_call x0 -> x4, Pallas kernels: none -> 8.15 us  [the longest x1 6.67 us: one_image(): pl.pallas_call(functools.partial(pair_kernel, sizes), out_shape=(jax.Shap...]
    reshape x3 -> x0, local copies, waits for them, and re-layouts: 4.52 us -> none  [the longest x1 1.94 us: image_terms(): pooled = jnp.einsum('chp,phd->chd', attn, patch_values, preferred_element...]
    unnamed x13 -> x8, local copies, waits for them, and re-layouts: 5.12 us -> 0.69 us
    transpose x2 -> x0, local copies, waits for them, and re-layouts: 3.96 us -> none  [the longest x1 1.99 us: image_terms(): jnp.einsum('chp,phd->chd', attn, patch_values, preferred_element_type=jnp...]
  transfers between devices with their start and end apart: 3 -> 1, of which waited for: 3 -> 1; matrix products, arithmetic and copies ran while one was open for 12% -> 0% of each run, Pallas kernels for 0% -> 0%
where the time goes in v2:
time: 88.5 us; the launch traced here: 88.1 us
  blocking collectives  60.9 us (69%)
  waiting for transfers between devices  10.7 us (12%)
  Pallas kernels  8.15 us (9%)
  starting transfers between devices  6.89 us (8%)
    all_to_all x3, blocking collectives, exchanged(): return lax.all_to_all(parts, axes, 0, 0, tiled=True)  60.9 us
    all_to_all x1, waiting for transfers between devices, exchanged(): return lax.all_to_all(parts, axes, 0, 0, tiled=True)  10.7 us
    all_to_all x1, starting transfers between devices, exchanged(): return lax.all_to_all(parts, axes, 0, 0, tiled=True)  6.89 us
    pallas_call x1, Pallas kernels, one_image(): pl.pallas_call(functools.partial(pair_kernel, sizes), out_shape=(jax.Shap...  6.67 us
  transfers between devices with their start and end apart: 1, of which 1 were waited for; matrix products, arithmetic and copies ran while one was open for 0% of the time, Pallas kernels for 0%

profile of v2, /device:TPU:1, one launch (start us, length us, event | category | flops | bytes accessed | tf_op | source)
XLA Modules:
  0.0 88.1 jit_solution(10599636307872206808)
XLA Ops:
  0.6 0.0 copy-start
  0.6 0.7 copy-done
  1.3 29.0 %all_to_all.20.cut_ref = bf16[32,4,128]{2,1,0:T(4,128)(2,1)S(1)} all-to-all(bf16[32,4,128]{2,1,0:T(4,128)(2,1)S(1)} %copies.1), channel_id=1, replica_groups=mesh['x_lo'=2,'core'=2,'x_hi'=2,'y'=4,'z'=16] {'core','z'}, dimensions={0} | all-to-all | bytes 65536 | tf_op jit(solution)/shard_map/all_to_all | solution.py:27
  30.3 0.9 rows.1
  31.2 0.0 copy-start.1
  31.2 0.0 copy-start.2
  31.2 0.0 copy-start.3
  31.2 6.9 %all-to-all-start.1 = ((bf16[16,32,512]{2,1,0:T(8,128)(2,1)}), bf16[16,32,512]{2,1,0:T(8,128)(2,1)S(1)}, u32[]{:S(2)}, u32[]{:S(2)}) async-start(bf16[16,32,512]{2,1,0:T(8,128)(2,1)} %rows.1), calls=%async_computation.1 | async-start | bytes 1048576 | tf_op jit(solution)/shard_map/all_to_all | solution.py:27
  38.1 10.7 %all-to-all-done.1 = bf16[16,32,512]{2,1,0:T(8,128)(2,1)S(1)} async-done(((bf16[16,32,512]{2,1,0:T(8,128)(2,1)}), bf16[16,32,512]{2,1,0:T(8,128)(2,1)S(1)}, u32[]{:S(2)}, u32[]{:S(2)}) %all-to-all-start.1) | async-done | bytes 524320 | tf_op jit(solution)/shard_map/all_to_all | solution.py:27
  48.8 0.0 copy-done.1
  48.8 0.0 copy-done.2
  48.8 0.0 copy-done.3
  48.8 6.7 %pairs.1 = (bf16[512,640]{1,0:T(8,128)(2,1)S(1)}, f32[784,128]{1,0:T(8,128)}, f32[784,128]{1,0:T(8,128)}) custom-call(s32[1]{0:T(128)} %bitcast.image_ref, s32[1,512]{1,0:T(1,128)S(1)} %bitcast.13, bf16[512,512]{1,0:T(8,128)(2,1)S(1)} %bitcast.10, bf16[196,512]{1,0:T(8,128)(2,1)S(1)} %bitcast.11, bf16[196,512]{1,0:T(8,128)(2,1)S(1)} %bitcast.12), custom_call_target="tpu_custom_call" | custom-call | flops 616562688 | bytes 3145728 | tf_op jit(solution)/shard_map/pairs/pallas_call | solution.py:212
  55.5 17.8 %all_to_all.21 = bf16[32,16,640]{2,1,0:T(8,128)(2,1)S(1)} all-to-all(bf16[32,16,640]{2,1,0:T(8,128)(2,1)S(1)} %bitcast.9), channel_id=1, replica_groups=mesh['x_lo'=2,'core'=2,'x_hi'=2,'y'=4,'z'=16] {'x_lo','x_hi','y','core'}, dimensions={0} | all-to-all | bytes 1310720 | tf_op jit(solution)/shard_map/all_to_all | solution.py:27
  73.3 0.1 convert_reduce_fusion
  73.4 14.1 %all_to_all.22.parts_ref = f32[16,1,640]{2,1,0:T(1,128)S(1)} all-to-all(f32[16,1,640]{2,1,0:T(1,128)S(1)} %broadcast_in_dim.3), channel_id=1, replica_groups=mesh['x_lo'=2,'core'=2,'x_hi'=2,'y'=4,'z'=16] {'z'}, dimensions={0} | all-to-all | bytes 81920 | tf_op jit(solution)/shard_map/all_to_all | solution.py:27
  87.5 0.6 total.1
  (2 shorter events, 0.0 us)
Async XLA Ops:
  0.6 0.7 copy-start
  31.2 17.6 %copy-start.1 = (bf16[1,196,512]{2,1,0:T(8,128)(2,1)S(1)}, bf16[1,196,512]{2,1,0:T(8,128)(2,1)}, u32[]{:S(2)}) copy-start(bf16[1,196,512]{2,1,0:T(8,128)(2,1)} %param.5) | copy-start | bytes 602116
  31.2 17.6 %copy-start.2 = (bf16[1,196,512]{2,1,0:T(8,128)(2,1)S(1)}, bf16[1,196,512]{2,1,0:T(8,128)(2,1)}, u32[]{:S(2)}) copy-start(bf16[1,196,512]{2,1,0:T(8,128)(2,1)} %param.6) | copy-start | bytes 602116
  31.2 17.6 %copy-start.3 = (s32[512]{0:T(512)S(1)}, s32[512]{0:T(512)}, u32[]{:S(2)}) copy-start(s32[512]{0:T(512)} %param.7) | copy-start | bytes 6148
  31.2 17.6 %all-to-all-start.1 = ((bf16[16,32,512]{2,1,0:T(8,128)(2,1)}), bf16[16,32,512]{2,1,0:T(8,128)(2,1)S(1)}, u32[]{:S(2)}, u32[]{:S(2)}) async-start(bf16[16,32,512]{2,1,0:T(8,128)(2,1)} %rows.1), calls=%async_computation.1 | async-start | bytes 1048576 | tf_op jit(solution)/shard_map/all_to_all | solution.py:27

commit v3 on v2

--- a/solution.py
+++ b/solution.py
@@ -72,10 +72,11 @@
     return exchanged(rows, PLANE).reshape(-1, width)
 
 
-def summed(rows, image_total, width):
-    plane = PLANE + LINE[:1]
-    parts = rows.reshape(lax.axis_size(plane), -1, rows.shape[1])
-    parts = jnp.sum(exchanged(parts, plane).astype(jnp.float32), axis=0)
+def summed(own, other, second, image_total, width):
+    both = lax.all_gather(other, LINE[0], axis=0)
+    swapped = jnp.where(second > 0, both[0], both[1])
+    parts = (own.astype(jnp.float32) + swapped.astype(jnp.float32)).astype(own.dtype)
+    parts = jnp.sum(exchanged(parts, PLANE).astype(jnp.float32), axis=0)
     parts = exchanged(parts[:, None], LINE[1:])
     inside = pl.BlockSpec(memory_space=pltpu.VMEM)
     return pl.pallas_call(
@@ -107,57 +108,57 @@
     return jnp.concatenate([rows, zeros] if head % 2 == 0 else [zeros, rows], axis=0)
 
 
-def pair_of(head, depth):
-    first = head // 2 * 2 * depth
-    return slice(first, first + 2 * depth)
-
-
 def pair_kernel(
-    sizes, image_ref, pairs_ref, text_ref, keys_ref, values_ref,
-    sums_ref, keys_out, values_out,
-    keys_t_in, values_t_in,
-    text_t, dout_t, attn, dscore, weights, pooled, grad_keys, grad_values, left,
+    sizes, pairs_ref, text_ref, keys_ref, values_ref,
+    own_ref, other_ref, second_ref, keys_out, values_out,
+    keys_t, values_t, text_t, dout_t, attn, dscore, weights, pooled, sums,
+    grad_keys, grad_values, pairs_in, arrived, left,
 ):
+    pairs_copy = pltpu.make_async_copy(pairs_ref, pairs_in, arrived)
+    pairs_copy.start()
     count, width = text_ref.shape
     patches = keys_ref.shape[0]
     depth = width // HEADS
     scale = depth ** (-0.5)
-    text_t[...] = text_ref[...].T
-    wide = text_t[...].astype(jnp.float32)
-    tnorm = lax.rsqrt(jnp.mean(wide * wide, 0, keepdims=True) + EPS)
-    values_t_in[...] = values_ref[...].T
-    for head in range(HEADS):
-        rows = slice(head * depth, (head + 1) * depth)
-        query = text_t[rows, :] * jnp.asarray(scale, jnp.bfloat16)
-        scores = jnp.dot(
-            keys_ref[:, pair_of(head, depth)],
-            padded_head(query, head),
-            preferred_element_type=jnp.float32,
-        )
-        grown = jnp.exp(scores - jnp.max(scores, 0, keepdims=True))
-        weight = grown * (1.0 / jnp.sum(grown, 0, keepdims=True))
-        weights[head] = weight
-        attn[head] = weight.astype(jnp.bfloat16)
-        pooled[rows, :] = jnp.dot(
-            values_t_in[rows, :], attn[head], preferred_element_type=jnp.float32
-        )
-    keys_t_in[...] = keys_ref[...].T
-    pool = pooled[...]
-    pnorm = lax.rsqrt(jnp.mean(pool * pool, 0, keepdims=True) + EPS)
-    cosine = jnp.mean(pool * wide, 0, keepdims=True) * pnorm * tnorm
+    blocks = HEADS // 2
+    text_square = pool_square = pool_text = jnp.zeros((1, count), jnp.float32)
+    for block in range(blocks):
+        lanes = slice(2 * block * depth, 2 * (block + 1) * depth)
+        text_t[lanes, :] = text_ref[:, lanes].T
+        values_t[lanes, :] = values_ref[:, lanes].T
+        for head in (2 * block, 2 * block + 1):
+            rows = slice(head * depth, (head + 1) * depth)
+            query = text_t[rows, :]
+            scores = jnp.dot(
+                keys_ref[:, lanes],
+                padded_head(query * jnp.asarray(scale, query.dtype), head),
+                preferred_element_type=jnp.float32,
+            )
+            grown = jnp.exp(scores - jnp.max(scores, 0, keepdims=True))
+            weight = grown * (1.0 / jnp.sum(grown, 0, keepdims=True))
+            weights[head] = weight
+            attn[head] = weight.astype(jnp.bfloat16)
+            pool = jnp.dot(values_t[rows, :], attn[head], preferred_element_type=jnp.float32)
+            pooled[rows, :] = pool
+            wide = query.astype(jnp.float32)
+            text_square += jnp.sum(wide * wide, 0, keepdims=True)
+            pool_square += jnp.sum(pool * pool, 0, keepdims=True)
+            pool_text += jnp.sum(pool * wide, 0, keepdims=True)
+    tnorm = lax.rsqrt(text_square * (1.0 / width) + EPS)
+    pnorm = lax.rsqrt(pool_square * (1.0 / width) + EPS)
+    cosine = pool_text * (1.0 / width) * pnorm * tnorm
     logit = LOGIT_SCALE * cosine + LOGIT_BIAS
     captions = lax.broadcasted_iota(jnp.int32, (1, count), 1)
-    described = jnp.where(pairs_ref[...] == image_ref[0], captions, 0)
+    pairs_copy.wait()
+    described = jnp.where(pairs_in[...] == lax.axis_index(OVER), captions, 0)
     matching = gathered_place(jnp.sum(described, 1, keepdims=True), sizes)
     label = jnp.where(captions == matching, 1.0, -1.0).astype(jnp.float32)
     margin = -label * logit
     loss = jnp.maximum(margin, 0.0) + jnp.log1p(jnp.exp(-jnp.abs(margin)))
     slope = -label / (1.0 + jnp.exp(-margin))
     dcos = LOGIT_SCALE / width * slope
-    dout_t[...] = (
-        (pnorm * dcos * tnorm) * wide - (pnorm * dcos * cosine * pnorm) * pool
-    ).astype(jnp.bfloat16)
-    pooled[...] = (tnorm * dcos * pnorm) * pool - (tnorm * dcos * cosine * tnorm) * wide
+    out_text, out_pool = pnorm * dcos * tnorm, pnorm * dcos * cosine * pnorm
+    direct_pool, direct_text = tnorm * dcos * pnorm, tnorm * dcos * cosine * tnorm
 
     def over_captions(parts, rows_t, head):
         return lax.dot_general(
@@ -167,22 +168,27 @@
             preferred_element_type=jnp.float32,
         )
 
-    blocks = HEADS // 2
+    parts = (sizes[0] * sizes[2] * sizes[3], sizes[1], sizes[4])
     for block in range(blocks):
-        lines = pl.ds(block, patches, stride=blocks)
+        lanes = slice(2 * block * depth, 2 * (block + 1) * depth)
+        keys_t[lanes, :] = keys_ref[:, lanes].T
         for head in (2 * block, 2 * block + 1):
             rows = slice(head * depth, (head + 1) * depth)
+            wide = text_t[rows, :].astype(jnp.float32)
+            pool = pooled[rows, :]
+            dout = (out_text * wide - out_pool * pool).astype(jnp.bfloat16)
+            dout_t[rows, :] = dout
             dattn = jnp.dot(
-                values_ref[:, pair_of(head, depth)],
-                padded_head(dout_t[rows, :], head),
-                preferred_element_type=jnp.float32,
+                values_ref[:, lanes], padded_head(dout, head), preferred_element_type=jnp.float32
             )
             weight = weights[head]
             carried = jnp.sum(weight * dattn, 0, keepdims=True)
             dscore[head] = (weight * scale * (dattn - carried)).astype(jnp.bfloat16)
-            pooled[rows, :] += jnp.dot(
-                keys_t_in[rows, :], dscore[head], preferred_element_type=jnp.float32
+            pooled[rows, :] = (direct_pool * pool - direct_text * wide) + jnp.dot(
+                keys_t[rows, :], dscore[head], preferred_element_type=jnp.float32
             )
+        sums[..., lanes] = pooled[lanes, :].T.astype(jnp.bfloat16).reshape(*parts, 2 * depth)
+        lines = pl.ds(block, patches, stride=blocks)
         grad_values[lines, :] = over_captions(attn, dout_t, 2 * block) + over_captions(
             attn, dout_t, 2 * block + 1
         )
@@ -193,34 +199,41 @@
     keys_copy = pltpu.make_async_copy(grad_keys, keys_out, left.at[1])
     values_copy.start()
     keys_copy.start()
-    sums_ref[:, :width] = pooled[...].T.astype(jnp.bfloat16)
-    sums_ref[:, width:] = jnp.broadcast_to(loss, (LOSS_LANES, count)).T.astype(jnp.bfloat16)
+    losses = jnp.broadcast_to(loss, (LOSS_LANES, count)).T.astype(jnp.bfloat16)
+    sums[..., width:] = losses.reshape(*parts, LOSS_LANES)
+    core = lax.axis_index(LINE[0])
+    own_ref[...] = sums[:, core]
+    other_ref[...] = sums[:, 1 - core]
+    second_ref[...] = jnp.full(second_ref.shape, core, jnp.float32)
     values_copy.wait()
     keys_copy.wait()
 
 
-def one_image(sizes, image, pairs, all_text, keys, values):
+def one_image(sizes, pairs, all_text, keys, values):
     patches, width = keys.shape[1:]
     count = all_text.shape[0]
     flops = 2 * count * patches * width
     lines = (patches * HEADS // 2, 2 * width // HEADS)
+    apart = (sizes[0] * sizes[2] * sizes[3], sizes[4], width + LOSS_LANES)
     inside = pl.BlockSpec(memory_space=pltpu.VMEM)
     anywhere = pl.BlockSpec(memory_space=pl.ANY)
     tall_text = pltpu.VMEM((width, count), jnp.bfloat16)
     tall_image = pltpu.VMEM((width, patches), jnp.bfloat16)
     per_head = pltpu.VMEM((HEADS, patches, count), jnp.bfloat16)
-    sums, grad_keys, grad_values = pl.pallas_call(
+    own, other, second, grad_keys, grad_values = pl.pallas_call(
         functools.partial(pair_kernel, sizes),
         out_shape=(
-            jax.ShapeDtypeStruct((count, width + LOSS_LANES), jnp.bfloat16),
+            jax.ShapeDtypeStruct(apart, jnp.bfloat16),
+            jax.ShapeDtypeStruct(apart, jnp.bfloat16),
+            jax.ShapeDtypeStruct((1, apart[2]), jnp.float32),
             jax.ShapeDtypeStruct(lines, jnp.float32),
             jax.ShapeDtypeStruct(lines, jnp.float32),
         ),
         in_specs=[
-            pl.BlockSpec(memory_space=pltpu.SMEM),
-            *[inside] * 4,
+            anywhere,
+            *[inside] * 3,
         ],
-        out_specs=(inside, anywhere, anywhere),
+        out_specs=(inside, inside, inside, anywhere, anywhere),
         scratch_shapes=[
             tall_image,
             tall_image,
@@ -230,8 +243,11 @@
             per_head,
             pltpu.VMEM((HEADS, patches, count), jnp.float32),
             pltpu.VMEM((width, count), jnp.float32),
+            pltpu.VMEM((apart[0], sizes[1], *apart[1:]), jnp.bfloat16),
             pltpu.VMEM(lines, jnp.float32),
             pltpu.VMEM(lines, jnp.float32),
+            pltpu.VMEM(pairs.shape, pairs.dtype),
+            pltpu.SemaphoreType.DMA(()),
             pltpu.SemaphoreType.DMA((2,)),
         ],
         compiler_params=pltpu.CompilerParams(vmem_limit_bytes=VMEM_BYTES),
@@ -239,24 +255,22 @@
             flops=6 * flops, bytes_accessed=3 << 20, transcendentals=HEADS * patches * count
         ),
         name="pairs",
-    )(image, pairs, all_text, keys[0], values[0])
-    return sums, grad_keys.reshape(keys.shape), grad_values.reshape(values.shape)
+    )(pltpu.with_memory_space_constraint(pairs, pltpu.HBM), all_text, keys[0], values[0])
+    return own, other, second, grad_keys.reshape(keys.shape), grad_values.reshape(values.shape)
 
 
 def local(text, keys, values, pair_image):
     width = text.shape[1]
-    image = lax.axis_index(OVER)
     image_total = lax.axis_size(OVER)
     all_text = gathered(text)
-    sums, grad_keys, grad_values = one_image(
+    own, other, second, grad_keys, grad_values = one_image(
         tuple(lax.axis_size(axis) for axis in OVER),
-        image.astype(jnp.int32).reshape(1),
         pair_image.reshape(1, -1),
         all_text,
         keys,
         values,
     )
-    loss, grad_text = summed(sums, image_total, width)
+    loss, grad_text = summed(own, other, second, image_total, width)
     return (loss.reshape(1), grad_text, grad_keys, grad_values)
 
 

time: 88.5 us -> 85.3 us (0.964)
  blocking collectives: 60.9 us -> 74.9 us
  waiting for transfers between devices: 10.7 us -> 0 us
  starting transfers between devices: 6.89 us -> 0 us
    all_to_all x1 -> x0, waiting for transfers between devices: 10.7 us -> none  [exchanged(): return lax.all_to_all(parts, axes, 0, 0, tiled=True)]
    all_to_all x3 -> x4, blocking collectives: 60.9 us -> 71.5 us  [exchanged(): return lax.all_to_all(parts, axes, 0, 0, tiled=True)]
    all_to_all x1 -> x0, starting transfers between devices: 6.89 us -> none  [exchanged(): return lax.all_to_all(parts, axes, 0, 0, tiled=True)]
    all_gather x0 -> x1, blocking collectives: none -> 3.32 us  [summed(): both = lax.all_gather(other, LINE[0], axis=0)]
  transfers between devices with their start and end apart: 1 -> 0, of which waited for: 1 -> 0; matrix products, arithmetic and copies ran while one was open for 0% -> 0% of each run, Pallas kernels for 0% -> 0%
where the time goes in v3:
time: 85.3 us; the launch traced here: 84.3 us
  blocking collectives  74.9 us (88%)
  Pallas kernels  7.88 us (9%)
    all_to_all x4, blocking collectives, exchanged(): return lax.all_to_all(parts, axes, 0, 0, tiled=True)  71.5 us
    pallas_call x1, Pallas kernels, one_image(): pl.pallas_call(functools.partial(pair_kernel, sizes), out_shape=(jax.Shap...  7.19 us
    all_gather x1, blocking collectives, summed(): both = lax.all_gather(other, LINE[0], axis=0)  3.32 us

profile of v3, /device:TPU:1, one launch (start us, length us, event | category | flops | bytes accessed | tf_op | source)
XLA Modules:
  0.0 84.3 jit_solution(13529227740389663035)
XLA Ops:
  0.6 0.0 copy-start
  0.6 0.7 copy-done
  1.3 29.0 %all_to_all.20.cut_ref = bf16[32,4,128]{2,1,0:T(4,128)(2,1)S(1)} all-to-all(bf16[32,4,128]{2,1,0:T(4,128)(2,1)S(1)} %copies.1), channel_id=1, replica_groups=mesh['x_lo'=2,'core'=2,'x_hi'=2,'y'=4,'z'=16] {'core','z'}, dimensions={0} | all-to-all | bytes 65536 | tf_op jit(solution)/shard_map/all_to_all | solution.py:27
  30.3 0.1 rows.1
  30.4 0.0 copy-start.1
  30.4 0.0 copy-start.2
  30.4 17.4 %all_to_all.21 = bf16[16,32,512]{2,1,0:T(8,128)(2,1)S(1)} all-to-all(bf16[16,32,512]{2,1,0:T(8,128)(2,1)S(1)} %rows.1), channel_id=1, replica_groups=mesh['x_lo'=2,'core'=2,'x_hi'=2,'y'=4,'z'=16] {'x_lo','x_hi','y'}, dimensions={0} | all-to-all | bytes 1048576 | tf_op jit(solution)/shard_map/all_to_all | solution.py:27
  47.8 0.0 copy-done.1
  47.8 0.0 copy-done.2
  47.8 7.2 %pairs.1 = (bf16[16,16,640]{2,1,0:T(8,128)(2,1)S(1)}, bf16[16,16,640]{2,1,0:T(8,128)(2,1)S(1)}, f32[1,640]{1,0:T(1,128)S(1)}, f32[784,128]{1,0:T(8,128)}, f32[784,128]{1,0:T(8,128)}) custom-call(s32[1,512]{1,0:T(1,128)} %bitcast.10, bf16[512,512]{1,0:T(8,128)(2,1)S(1)} %bitcast.7, bf16[196,512]{1,0:T(8,128)(2,1)S(1)} %bitcast.8, bf16[196,512]{1,0:T(8,128)(2,1)S(1)} %bitcast.9), custom_call_target="tpu_custom_call" | custom-call | flops 616562688 | bytes 3145728 | tf_op jit(solution)/shard_map/pairs/pallas_call | solution.py:223
  55.0 3.3 %all-gather = bf16[32,16,640]{2,1,0:T(8,128)(2,1)S(1)} all-gather(bf16[16,16,640]{2,1,0:T(8,128)(2,1)S(1)} %get-tuple-element.13), channel_id=2, replica_groups=mesh['x_lo'=2,'core'=2,'x_hi'=2,'y'=4,'z'=16] {'core'}, dimensions={0}, use_global_device_ids=true | all-gather | bytes 983040 | tf_op jit(solution)/shard_map/all_gather | solution.py:76
  58.4 0.1 add_convert_fusion
  58.5 11.1 %all_to_all.22 = bf16[16,16,640]{2,1,0:T(8,128)(2,1)S(1)} all-to-all(bf16[16,16,640]{2,1,0:T(8,128)(2,1)S(1)} %add_convert_fusion), channel_id=1, replica_groups=mesh['x_lo'=2,'core'=2,'x_hi'=2,'y'=4,'z'=16] {'x_lo','x_hi','y'}, dimensions={0} | all-to-all | bytes 655360 | tf_op jit(solution)/shard_map/all_to_all | solution.py:27
  69.6 0.1 convert_reduce_fusion
  69.7 14.0 %all_to_all.23.parts_ref = f32[16,1,640]{2,1,0:T(1,128)S(1)} all-to-all(f32[16,1,640]{2,1,0:T(1,128)S(1)} %broadcast_in_dim.12), channel_id=1, replica_groups=mesh['x_lo'=2,'core'=2,'x_hi'=2,'y'=4,'z'=16] {'z'}, dimensions={0} | all-to-all | bytes 81920 | tf_op jit(solution)/shard_map/all_to_all | solution.py:27
  83.7 0.6 total.1
  (3 shorter events, 0.1 us)
Async XLA Ops:
  0.6 0.7 copy-start
  30.4 17.4 %copy-start.1 = (bf16[1,196,512]{2,1,0:T(8,128)(2,1)S(1)}, bf16[1,196,512]{2,1,0:T(8,128)(2,1)}, u32[]{:S(2)}) copy-start(bf16[1,196,512]{2,1,0:T(8,128)(2,1)} %param.5) | copy-start | bytes 602116
  30.4 17.4 %copy-start.2 = (bf16[1,196,512]{2,1,0:T(8,128)(2,1)S(1)}, bf16[1,196,512]{2,1,0:T(8,128)(2,1)}, u32[]{:S(2)}) copy-start(bf16[1,196,512]{2,1,0:T(8,128)(2,1)} %param.6) | copy-start | bytes 602116

commit v4 on v3

--- a/solution.py
+++ b/solution.py
@@ -122,28 +122,39 @@
     scale = depth ** (-0.5)
     blocks = HEADS // 2
     text_square = pool_square = pool_text = jnp.zeros((1, count), jnp.float32)
-    for block in range(blocks):
-        lanes = slice(2 * block * depth, 2 * (block + 1) * depth)
-        text_t[lanes, :] = text_ref[:, lanes].T
-        values_t[lanes, :] = values_ref[:, lanes].T
-        for head in (2 * block, 2 * block + 1):
-            rows = slice(head * depth, (head + 1) * depth)
-            query = text_t[rows, :]
-            scores = jnp.dot(
-                keys_ref[:, lanes],
-                padded_head(query * jnp.asarray(scale, query.dtype), head),
-                preferred_element_type=jnp.float32,
-            )
-            grown = jnp.exp(scores - jnp.max(scores, 0, keepdims=True))
+    def rows_of(head):
+        return slice(head * depth, (head + 1) * depth)
+
+    def lanes_of(head):
+        return slice(head // 2 * 2 * depth, (head // 2 + 1) * 2 * depth)
+
+    def scored(head):
+        lanes = lanes_of(head)
+        if head % 2 == 0:
+            text_t[lanes, :] = text_ref[:, lanes].T
+            values_t[lanes, :] = values_ref[:, lanes].T
+        query = text_t[rows_of(head), :]
+        return jnp.dot(
+            keys_ref[:, lanes],
+            padded_head(query * jnp.asarray(scale, query.dtype), head),
+            preferred_element_type=jnp.float32,
+        )
+
+    scores = [scored(head) for head in range(HEADS)]
+    for head in range(HEADS + 1):
+        if head > 0:
+            rows = rows_of(head - 1)
+            pool = jnp.dot(values_t[rows, :], attn[head - 1], preferred_element_type=jnp.float32)
+            pooled[rows, :] = pool
+            wide = text_t[rows, :].astype(jnp.float32)
+            text_square += jnp.sum(wide * wide, 0, keepdims=True)
+            pool_square += jnp.sum(pool * pool, 0, keepdims=True)
+            pool_text += jnp.sum(pool * wide, 0, keepdims=True)
+        if head < HEADS:
+            grown = jnp.exp(scores[head] - jnp.max(scores[head], 0, keepdims=True))
             weight = grown * (1.0 / jnp.sum(grown, 0, keepdims=True))
             weights[head] = weight
             attn[head] = weight.astype(jnp.bfloat16)
-            pool = jnp.dot(values_t[rows, :], attn[head], preferred_element_type=jnp.float32)
-            pooled[rows, :] = pool
-            wide = query.astype(jnp.float32)
-            text_square += jnp.sum(wide * wide, 0, keepdims=True)
-            pool_square += jnp.sum(pool * pool, 0, keepdims=True)
-            pool_text += jnp.sum(pool * wide, 0, keepdims=True)
     tnorm = lax.rsqrt(text_square * (1.0 / width) + EPS)
     pnorm = lax.rsqrt(pool_square * (1.0 / width) + EPS)
     cosine = pool_text * (1.0 / width) * pnorm * tnorm
@@ -169,32 +180,41 @@
         )
 
     parts = (sizes[0] * sizes[2] * sizes[3], sizes[1], sizes[4])
-    for block in range(blocks):
-        lanes = slice(2 * block * depth, 2 * (block + 1) * depth)
-        keys_t[lanes, :] = keys_ref[:, lanes].T
-        for head in (2 * block, 2 * block + 1):
-            rows = slice(head * depth, (head + 1) * depth)
-            wide = text_t[rows, :].astype(jnp.float32)
-            pool = pooled[rows, :]
-            dout = (out_text * wide - out_pool * pool).astype(jnp.bfloat16)
-            dout_t[rows, :] = dout
-            dattn = jnp.dot(
-                values_ref[:, lanes], padded_head(dout, head), preferred_element_type=jnp.float32
+    def attended(head):
+        lanes, rows = lanes_of(head), rows_of(head)
+        if head % 2 == 0:
+            keys_t[lanes, :] = keys_ref[:, lanes].T
+        wide = text_t[rows, :].astype(jnp.float32)
+        pool = pooled[rows, :]
+        dout = (out_text * wide - out_pool * pool).astype(jnp.bfloat16)
+        dout_t[rows, :] = dout
+        pooled[rows, :] = direct_pool * pool - direct_text * wide
+        return jnp.dot(
+            values_ref[:, lanes], padded_head(dout, head), preferred_element_type=jnp.float32
+        )
+
+    dattn = [attended(head) for head in range(HEADS)]
+    for head in range(HEADS + 1):
+        if head > 0:
+            rows = rows_of(head - 1)
+            pooled[rows, :] += jnp.dot(
+                keys_t[rows, :], dscore[head - 1], preferred_element_type=jnp.float32
             )
+        if head > 0 and head % 2 == 0:
+            block = head // 2 - 1
+            lanes = lanes_of(head - 1)
+            sums[..., lanes] = pooled[lanes, :].T.astype(jnp.bfloat16).reshape(*parts, 2 * depth)
+            lines = pl.ds(block, patches, stride=blocks)
+            grad_values[lines, :] = over_captions(attn, dout_t, 2 * block) + over_captions(
+                attn, dout_t, 2 * block + 1
+            )
+            grad_keys[lines, :] = over_captions(dscore, text_t, 2 * block) + over_captions(
+                dscore, text_t, 2 * block + 1
+            )
+        if head < HEADS:
             weight = weights[head]
-            carried = jnp.sum(weight * dattn, 0, keepdims=True)
-            dscore[head] = (weight * scale * (dattn - carried)).astype(jnp.bfloat16)
-            pooled[rows, :] = (direct_pool * pool - direct_text * wide) + jnp.dot(
-                keys_t[rows, :], dscore[head], preferred_element_type=jnp.float32
-            )
-        sums[..., lanes] = pooled[lanes, :].T.astype(jnp.bfloat16).reshape(*parts, 2 * depth)
-        lines = pl.ds(block, patches, stride=blocks)
-        grad_values[lines, :] = over_captions(attn, dout_t, 2 * block) + over_captions(
-            attn, dout_t, 2 * block + 1
-        )
-        grad_keys[lines, :] = over_captions(dscore, text_t, 2 * block) + over_captions(
-            dscore, text_t, 2 * block + 1
-        )
+            carried = jnp.sum(weight * dattn[head], 0, keepdims=True)
+            dscore[head] = (weight * scale * (dattn[head] - carried)).astype(jnp.bfloat16)
     values_copy = pltpu.make_async_copy(grad_values, values_out, left.at[0])
     keys_copy = pltpu.make_async_copy(grad_keys, keys_out, left.at[1])
     values_copy.start()

time: 85.3 us -> 83 us (0.973)
  Pallas kernels: 7.88 us -> 5.53 us
    pallas_call x1, Pallas kernels: 7.19 us -> 4.84 us  [one_image(): pl.pallas_call(functools.partial(pair_kernel, sizes), out_shape=(jax.Shap...]
where the time goes in v4:
time: 83 us; the launch traced here: 82 us
  blocking collectives  74.8 us (90%)
  Pallas kernels  5.53 us (7%)
    all_to_all x4, blocking collectives, exchanged(): return lax.all_to_all(parts, axes, 0, 0, tiled=True)  71.5 us
    pallas_call x1, Pallas kernels, one_image(): pl.pallas_call(functools.partial(pair_kernel, sizes), out_shape=(jax.Shap...  4.84 us
    all_gather x1, blocking collectives, summed(): both = lax.all_gather(other, LINE[0], axis=0)  3.3 us

profile of v4, /device:TPU:1, one launch (start us, length us, event | category | flops | bytes accessed | tf_op | source)
XLA Modules:
  0.0 82.0 jit_solution(12402449141456195442)
XLA Ops:
  0.6 0.0 copy-start
  0.6 0.7 copy-done
  1.3 29.0 %all_to_all.20.cut_ref = bf16[32,4,128]{2,1,0:T(4,128)(2,1)S(1)} all-to-all(bf16[32,4,128]{2,1,0:T(4,128)(2,1)S(1)} %copies.1), channel_id=1, replica_groups=mesh['x_lo'=2,'core'=2,'x_hi'=2,'y'=4,'z'=16] {'core','z'}, dimensions={0} | all-to-all | bytes 65536 | tf_op jit(solution)/shard_map/all_to_all | solution.py:27
  30.3 0.1 rows.1
  30.4 0.0 copy-start.1
  30.4 0.0 copy-start.2
  30.4 17.4 %all_to_all.21 = bf16[16,32,512]{2,1,0:T(8,128)(2,1)S(1)} all-to-all(bf16[16,32,512]{2,1,0:T(8,128)(2,1)S(1)} %rows.1), channel_id=1, replica_groups=mesh['x_lo'=2,'core'=2,'x_hi'=2,'y'=4,'z'=16] {'x_lo','x_hi','y'}, dimensions={0} | all-to-all | bytes 1048576 | tf_op jit(solution)/shard_map/all_to_all | solution.py:27
  47.8 0.0 copy-done.1
  47.8 0.0 copy-done.2
  47.8 4.8 %pairs.1 = (bf16[16,16,640]{2,1,0:T(8,128)(2,1)S(1)}, bf16[16,16,640]{2,1,0:T(8,128)(2,1)S(1)}, f32[1,640]{1,0:T(1,128)S(1)}, f32[784,128]{1,0:T(8,128)}, f32[784,128]{1,0:T(8,128)}) custom-call(s32[1,512]{1,0:T(1,128)} %bitcast.10, bf16[512,512]{1,0:T(8,128)(2,1)S(1)} %bitcast.7, bf16[196,512]{1,0:T(8,128)(2,1)S(1)} %bitcast.8, bf16[196,512]{1,0:T(8,128)(2,1)S(1)} %bitcast.9), custom_call_target="tpu_custom_call" | custom-call | flops 616562688 | bytes 3145728 | tf_op jit(solution)/shard_map/pairs/pallas_call | solution.py:243
  52.7 3.3 %all-gather = bf16[32,16,640]{2,1,0:T(8,128)(2,1)S(1)} all-gather(bf16[16,16,640]{2,1,0:T(8,128)(2,1)S(1)} %get-tuple-element.13), channel_id=2, replica_groups=mesh['x_lo'=2,'core'=2,'x_hi'=2,'y'=4,'z'=16] {'core'}, dimensions={0}, use_global_device_ids=true | all-gather | bytes 983040 | tf_op jit(solution)/shard_map/all_gather | solution.py:76
  56.0 0.1 add_convert_fusion
  56.1 11.1 %all_to_all.22 = bf16[16,16,640]{2,1,0:T(8,128)(2,1)S(1)} all-to-all(bf16[16,16,640]{2,1,0:T(8,128)(2,1)S(1)} %add_convert_fusion), channel_id=1, replica_groups=mesh['x_lo'=2,'core'=2,'x_hi'=2,'y'=4,'z'=16] {'x_lo','x_hi','y'}, dimensions={0} | all-to-all | bytes 655360 | tf_op jit(solution)/shard_map/all_to_all | solution.py:27
  67.3 0.1 convert_reduce_fusion
  67.3 14.0 %all_to_all.23.parts_ref = f32[16,1,640]{2,1,0:T(1,128)S(1)} all-to-all(f32[16,1,640]{2,1,0:T(1,128)S(1)} %broadcast_in_dim.12), channel_id=1, replica_groups=mesh['x_lo'=2,'core'=2,'x_hi'=2,'y'=4,'z'=16] {'z'}, dimensions={0} | all-to-all | bytes 81920 | tf_op jit(solution)/shard_map/all_to_all | solution.py:27
  81.4 0.6 total.1
  (3 shorter events, 0.1 us)
Async XLA Ops:
  0.6 0.7 copy-start
  30.4 17.4 %copy-start.1 = (bf16[1,196,512]{2,1,0:T(8,128)(2,1)S(1)}, bf16[1,196,512]{2,1,0:T(8,128)(2,1)}, u32[]{:S(2)}) copy-start(bf16[1,196,512]{2,1,0:T(8,128)(2,1)} %param.5) | copy-start | bytes 602116
  30.4 17.4 %copy-start.2 = (bf16[1,196,512]{2,1,0:T(8,128)(2,1)S(1)}, bf16[1,196,512]{2,1,0:T(8,128)(2,1)}, u32[]{:S(2)}) copy-start(bf16[1,196,512]{2,1,0:T(8,128)(2,1)} %param.6) | copy-start | bytes 602116

commit v5 on v4

--- a/solution.py
+++ b/solution.py
@@ -110,9 +110,9 @@
 
 def pair_kernel(
     sizes, pairs_ref, text_ref, keys_ref, values_ref,
-    own_ref, other_ref, second_ref, keys_out, values_out,
+    own_ref, other_ref, second_ref, grad_keys, grad_values,
     keys_t, values_t, text_t, dout_t, attn, dscore, weights, pooled, sums,
-    grad_keys, grad_values, pairs_in, arrived, left,
+    pairs_in, arrived,
 ):
     pairs_copy = pltpu.make_async_copy(pairs_ref, pairs_in, arrived)
     pairs_copy.start()
@@ -208,25 +208,24 @@
             grad_values[lines, :] = over_captions(attn, dout_t, 2 * block) + over_captions(
                 attn, dout_t, 2 * block + 1
             )
-            grad_keys[lines, :] = over_captions(dscore, text_t, 2 * block) + over_captions(
-                dscore, text_t, 2 * block + 1
+            first = lax.broadcasted_iota(jnp.int32, (1, 2 * depth), 1) < depth
+            near, far = (
+                jnp.dot(
+                    dscore[2 * block + k], text_ref[:, lanes], preferred_element_type=jnp.float32
+                )
+                for k in range(2)
             )
+            grad_keys[lines, :] = jnp.where(first, near, far)
         if head < HEADS:
             weight = weights[head]
             carried = jnp.sum(weight * dattn[head], 0, keepdims=True)
             dscore[head] = (weight * scale * (dattn[head] - carried)).astype(jnp.bfloat16)
-    values_copy = pltpu.make_async_copy(grad_values, values_out, left.at[0])
-    keys_copy = pltpu.make_async_copy(grad_keys, keys_out, left.at[1])
-    values_copy.start()
-    keys_copy.start()
     losses = jnp.broadcast_to(loss, (LOSS_LANES, count)).T.astype(jnp.bfloat16)
     sums[..., width:] = losses.reshape(*parts, LOSS_LANES)
     core = lax.axis_index(LINE[0])
     own_ref[...] = sums[:, core]
     other_ref[...] = sums[:, 1 - core]
     second_ref[...] = jnp.full(second_ref.shape, core, jnp.float32)
-    values_copy.wait()
-    keys_copy.wait()
 
 
 def one_image(sizes, pairs, all_text, keys, values):
@@ -253,7 +252,7 @@
             anywhere,
             *[inside] * 3,
         ],
-        out_specs=(inside, inside, inside, anywhere, anywhere),
+        out_specs=(inside,) * 5,
         scratch_shapes=[
             tall_image,
             tall_image,
@@ -264,11 +263,8 @@
             pltpu.VMEM((HEADS, patches, count), jnp.float32),
             pltpu.VMEM((width, count), jnp.float32),
             pltpu.VMEM((apart[0], sizes[1], *apart[1:]), jnp.bfloat16),
-            pltpu.VMEM(lines, jnp.float32),
-            pltpu.VMEM(lines, jnp.float32),
             pltpu.VMEM(pairs.shape, pairs.dtype),
             pltpu.SemaphoreType.DMA(()),
-            pltpu.SemaphoreType.DMA((2,)),
         ],
         compiler_params=pltpu.CompilerParams(vmem_limit_bytes=VMEM_BYTES),
         cost_estimate=pl.CostEstimate(

time: 83 us -> 82.9 us (level)
  no operation moved by 1% of the time
where the time goes in v5:
time: 82.9 us; the launch traced here: 81.9 us
  blocking collectives  74.9 us (90%)
  Pallas kernels  5.46 us (7%)
    all_to_all x4, blocking collectives, exchanged(): return lax.all_to_all(parts, axes, 0, 0, tiled=True)  71.5 us
    pallas_call x1, Pallas kernels, one_image(): pl.pallas_call(functools.partial(pair_kernel, sizes), out_shape=(jax.Shap...  4.78 us
    all_gather x1, blocking collectives, summed(): both = lax.all_gather(other, LINE[0], axis=0)  3.32 us

profile of v5, /device:TPU:1, one launch (start us, length us, event | category | flops | bytes accessed | tf_op | source)
XLA Modules:
  0.0 81.9 jit_solution(5584818628392234200)
XLA Ops:
  0.6 0.0 copy-start
  0.6 0.7 copy-done
  1.3 29.0 %all_to_all.20.cut_ref = bf16[32,4,128]{2,1,0:T(4,128)(2,1)S(1)} all-to-all(bf16[32,4,128]{2,1,0:T(4,128)(2,1)S(1)} %copies.1), channel_id=1, replica_groups=mesh['x_lo'=2,'core'=2,'x_hi'=2,'y'=4,'z'=16] {'core','z'}, dimensions={0} | all-to-all | bytes 65536 | tf_op jit(solution)/shard_map/all_to_all | solution.py:27
  30.3 0.1 rows.1
  30.4 0.0 copy-start.1
  30.4 0.0 copy-start.2
  30.4 17.4 %all_to_all.21 = bf16[16,32,512]{2,1,0:T(8,128)(2,1)S(1)} all-to-all(bf16[16,32,512]{2,1,0:T(8,128)(2,1)S(1)} %rows.1), channel_id=1, replica_groups=mesh['x_lo'=2,'core'=2,'x_hi'=2,'y'=4,'z'=16] {'x_lo','x_hi','y'}, dimensions={0} | all-to-all | bytes 1048576 | tf_op jit(solution)/shard_map/all_to_all | solution.py:27
  47.8 0.0 copy-done.1
  47.8 0.0 copy-done.2
  47.8 4.8 %pairs.1 = (bf16[16,16,640]{2,1,0:T(8,128)(2,1)S(1)}, bf16[16,16,640]{2,1,0:T(8,128)(2,1)S(1)}, f32[1,640]{1,0:T(1,128)S(1)}, f32[784,128]{1,0:T(8,128)}, f32[784,128]{1,0:T(8,128)}) custom-call(s32[1,512]{1,0:T(1,128)} %bitcast.10, bf16[512,512]{1,0:T(8,128)(2,1)S(1)} %bitcast.7, bf16[196,512]{1,0:T(8,128)(2,1)S(1)} %bitcast.8, bf16[196,512]{1,0:T(8,128)(2,1)S(1)} %bitcast.9), custom_call_target="tpu_custom_call" | custom-call | flops 616562688 | bytes 3145728 | tf_op jit(solution)/shard_map/pairs/pallas_call | solution.py:242
  52.6 3.3 %all-gather = bf16[32,16,640]{2,1,0:T(8,128)(2,1)S(1)} all-gather(bf16[16,16,640]{2,1,0:T(8,128)(2,1)S(1)} %get-tuple-element.13), channel_id=2, replica_groups=mesh['x_lo'=2,'core'=2,'x_hi'=2,'y'=4,'z'=16] {'core'}, dimensions={0}, use_global_device_ids=true | all-gather | bytes 983040 | tf_op jit(solution)/shard_map/all_gather | solution.py:76
  55.9 0.1 add_convert_fusion
  56.1 11.1 %all_to_all.22 = bf16[16,16,640]{2,1,0:T(8,128)(2,1)S(1)} all-to-all(bf16[16,16,640]{2,1,0:T(8,128)(2,1)S(1)} %add_convert_fusion), channel_id=1, replica_groups=mesh['x_lo'=2,'core'=2,'x_hi'=2,'y'=4,'z'=16] {'x_lo','x_hi','y'}, dimensions={0} | all-to-all | bytes 655360 | tf_op jit(solution)/shard_map/all_to_all | solution.py:27
  67.2 0.1 convert_reduce_fusion
  67.3 14.0 %all_to_all.23.parts_ref = f32[16,1,640]{2,1,0:T(1,128)S(1)} all-to-all(f32[16,1,640]{2,1,0:T(1,128)S(1)} %broadcast_in_dim.12), channel_id=1, replica_groups=mesh['x_lo'=2,'core'=2,'x_hi'=2,'y'=4,'z'=16] {'z'}, dimensions={0} | all-to-all | bytes 81920 | tf_op jit(solution)/shard_map/all_to_all | solution.py:27
  81.3 0.6 total.1
  (3 shorter events, 0.1 us)
Async XLA Ops:
  0.6 0.7 copy-start
  30.4 17.4 %copy-start.1 = (bf16[1,196,512]{2,1,0:T(8,128)(2,1)S(1)}, bf16[1,196,512]{2,1,0:T(8,128)(2,1)}, u32[]{:S(2)}) copy-start(bf16[1,196,512]{2,1,0:T(8,128)(2,1)} %param.5) | copy-start | bytes 602116
  30.4 17.4 %copy-start.2 = (bf16[1,196,512]{2,1,0:T(8,128)(2,1)S(1)}, bf16[1,196,512]{2,1,0:T(8,128)(2,1)}, u32[]{:S(2)}) copy-start(bf16[1,196,512]{2,1,0:T(8,128)(2,1)} %param.6) | copy-start | bytes 602116
